TPU v7x, 1024 devices: a whole 8x8x8 slice. The times are simulated.
1024 devices in a mesh: grid: 32 (over y_lo, z, core), band: 32 (over y_hi, x).
Axes of the slice: x: 8, y: 8 (y_hi: 4, y_lo: 2; y = y_hi * 2 + y_lo), z: 8, core: 2. Of those that a mesh axis runs over, the one named last changes fastest.
Arguments:
- orbitals: bfloat16 [32768, 4096], P('grid', 'band'), may hold values from -6 to 6
- points: int32 [4096], replicated, may hold values from 0 to 32767, as said below
- theta: bfloat16 [32768, 4096], P('grid'), may hold values from -0.09375 to 0.09375
- metric: float32 [4096, 4096], P('grid', 'band'), may hold values from -0.09375 to 0.09375
Outputs:
- applied: bfloat16 [32768, 4096], P('grid', 'band')
Inputs may be any that keep to these rules, and one draw needn't show every extreme that they name: The 4096 points are distinct grid indices in random order; every block of 1024 consecutive grid indices holds the same number of them.
All inputs are finite; a program needn't handle non-finite values.
Results may differ from a plain program's by a relative error of at most 0.0057.
Values may be sent and summed in bfloat16 or wider, within the bound.
No kernel may reach another device: no remote copies, remote signals or barrier semaphores. Data moves between devices by JAX's collectives and lax.ppermute only.
A program may use at most 64 MiB of HBM per device.

v0:
```python
import jax
import jax.numpy as jnp
from jax import lax
from jax.sharding import PartitionSpec as P

NB = 4096


def shards(orbitals, points, theta, metric):
    row_count = orbitals.shape[0]
    point_count = points.shape[0]
    grid_index = lax.axis_index("grid")
    per_device = point_count // lax.axis_size("grid")
    owners = points // row_count
    by_owner = jnp.argsort(owners, stable=True)
    my_slots = lax.dynamic_slice_in_dim(by_owner, grid_index * per_device, per_device, 0)
    my_rows = jnp.take(points, my_slots, axis=0) - grid_index * row_count
    packed = jnp.take(orbitals, my_rows, axis=0)
    gathered = lax.all_gather(packed, "grid", axis=0, tiled=True)
    placing = (
        jnp.zeros((point_count,), jnp.int32)
        .at[by_owner]
        .set(jnp.arange(point_count, dtype=jnp.int32))
    )
    sampled = jnp.take(gathered, placing, axis=0)
    my_points = lax.dynamic_slice_in_dim(sampled, grid_index * per_device, per_device, 0)
    partial_rows = lax.dot_general(
        my_points, sampled, (((1,), (1,)), ((), ())), preferred_element_type=jnp.float32
    )
    density = lax.psum(partial_rows, "band") * (1.0 / NB)
    squared = density * density
    kernel_part = jnp.dot(
        squared,
        lax.all_gather(metric, "grid", axis=0, tiled=True),
        precision=lax.Precision.HIGHEST,
        preferred_element_type=jnp.float32,
    )
    kernel = lax.all_gather(kernel_part.astype(jnp.bfloat16), "band", axis=1, tiled=True)
    coeffs = jnp.dot(kernel, sampled, preferred_element_type=jnp.float32).astype(jnp.bfloat16)
    applied = jnp.dot(
        theta,
        lax.all_gather(coeffs, "grid", axis=0, tiled=True),
        preferred_element_type=jnp.float32,
    )
    return applied.astype(jnp.bfloat16)


def solution(mesh):
    placed = (P("grid", "band"), P(), P("grid", None), P("grid", "band"))
    return jax.shard_map(
        shards, mesh=mesh, in_specs=placed, out_specs=P("grid", "band"), check_vma=False
    )
```

profile of v0, /device:TPU:1, one launch (start us, length us, event | category | flops | bytes accessed | tf_op | source)
XLA Modules:
  0.0 677.8 jit_solution(1763330514082831870)
XLA Ops:
  6.5 0.0 copy-start
  6.5 0.0 all-gather.5.cloned.1.call-start
  6.5 0.8 add_select_fusion
  7.3 5.8 sort.17
  13.1 0.1 compare_select_fusion.3
  13.2 1.6 gather_fusion
  14.8 0.1 compare_and_fusion.1
  14.9 0.0 copy-done
  14.9 0.7 gather_fusion.1
  15.7 0.7 broadcast_select_fusion.1
  16.4 0.0 all-gather.5.cloned.1.call-update
  16.4 0.0 all-gather.7.cloned.1.call-start
  16.4 0.7 all-gather.7.cloned.1.call-update
  17.1 0.0 all-reduce.2.cloned.1.call-start
  17.2 15.5 %scatter_custom_fusion = s32[4096]{0:T(1024)S(1)} fusion(s32[4096]{0:T(1024)S(1)} %compare_select_fusion.1, s32[4096]{0:T(1024)S(1)} %iota.8, s32[]{:T(128)} %constant.56.clone.1), kind=kCustom, calls=%fused_computation.27 | custom fusion | bytes 16388 | tf_op jit(solution)/shard_map/scatter | solution.py:23
  32.8 66.4 %all-gather.5.cloned.1.call-done = bf16[4096,128]{1,0:T(8,128)(2,1)} async-done(((bf16[128,128]{1,0:T(8,128)(2,1)}), bf16[4096,128]{1,0:T(8,128)(2,1)}) %all-gather.5.cloned.1.call-update) | async-done | bytes 1048592 | tf_op jit(solution)/shard_map/all_gather | solution.py:19
  99.2 12.4 %gather_fusion.2 = bf16[4096,128]{1,0:T(8,128)(2,1)S(1)} fusion(bf16[4096,128]{1,0:T(8,128)(2,1)} %all-gather.5.cloned.1.call-done, s32[4096]{0:T(1024)S(1)} %fusion.12), kind=kCustom, calls=%fused_computation.2 | custom fusion | bytes 2113536 | tf_op jit(solution)/shard_map/jit(_take)/gather | solution.py:25
  111.6 2.1 broadcast_select_fusion
  113.7 1.8 fusion.8
  115.5 0.0 all-reduce.2.cloned.1.call-update
  115.5 0.0 all-gather.9.cloned.1.call-start
  115.6 56.5 %all-gather.7.cloned.1.call-done = f32[4096,128]{1,0:T(8,128)} async-done(((f32[128,128]{1,0:T(8,128)}), f32[4096,128]{1,0:T(8,128)}) %all-gather.7.cloned.1.call-update) | async-done | bytes 2097168 | tf_op jit(solution)/shard_map/all_gather | solution.py:34
  172.0 312.0 %all-reduce.2.cloned.1.call-done = f32[128,4096]{1,0:T(8,128)} async-done(((f32[128,4096]{1,0:T(8,128)}), f32[128,4096]{1,0:T(8,128)}) %all-reduce.2.cloned.1.call-update) | async-done | bytes 2097168 | tf_op jit(solution)/shard_map/psum | solution.py:30
  484.0 5.1 fusion.4
  489.1 0.0 all-gather.9.cloned.1.call-update
  489.1 0.0 all-gather.11.cloned.1.call-start
  489.2 101.2 %all-gather.9.cloned.1.call-done = bf16[128,4096]{1,0:T(8,128)(2,1)} async-done(((bf16[128,128]{1,0:T(8,128)(2,1)}), bf16[128,4096]{1,0:T(8,128)(2,1)}) %all-gather.9.cloned.1.call-update) | async-done | bytes 1048592 | tf_op jit(solution)/shard_map/all_gather | solution.py:38
  590.3 2.3 convolution_convert_fusion.1
  592.6 0.0 all-gather.11.cloned.1.call-update
  592.6 71.2 %all-gather.11.cloned.1.call-done = bf16[4096,128]{1,0:T(8,128)(2,1)} async-done(((bf16[128,128]{1,0:T(8,128)(2,1)}), bf16[4096,128]{1,0:T(8,128)(2,1)}) %all-gather.11.cloned.1.call-update) | async-done | bytes 1048592 | tf_op jit(solution)/shard_map/all_gather | solution.py:42
  663.8 6.6 fusion.3
  670.5 0.8 copy.6
  (7 shorter events, 0.0 us)
Async XLA Ops:
  6.5 8.4 %copy-start = (bf16[1024,128]{1,0:T(8,128)(2,1)S(1)}, bf16[1024,128]{1,0:T(8,128)(2,1)}, u32[]{:S(2)}) copy-start(bf16[1024,128]{1,0:T(8,128)(2,1)} %param.4) | copy-start | bytes 786436
  6.5 92.6 %all-gather.5.cloned.1.call-start = ((), (), s32[]{:S(2)}) async-start(), calls=%async_computation | async-start | bytes 1081344 | tf_op jit(solution)/shard_map/all_gather | solution.py:19
  16.4 155.7 %all-gather.7.cloned.1.call-start = ((), (), s32[]{:S(2)}) async-start(), calls=%async_computation.2 | async-start | bytes 2162688 | tf_op jit(solution)/shard_map/all_gather | solution.py:34
  17.1 466.9 %all-reduce.2.cloned.1.call-start = ((), (), s32[]{:S(2)}) async-start(), calls=%async_computation.1 | async-start | bytes 4194304 | tf_op jit(solution)/shard_map/psum | solution.py:30
  115.5 474.8 %all-gather.9.cloned.1.call-start = ((), (), s32[]{:S(2)}) async-start(), calls=%async_computation.3 | async-start | bytes 1081344 | tf_op jit(solution)/shard_map/all_gather | solution.py:38
  489.1 174.7 %all-gather.11.cloned.1.call-start = ((), (), s32[]{:S(2)}) async-start(), calls=%async_computation.4 | async-start | bytes 1081344 | tf_op jit(solution)/shard_map/all_gather | solution.py:42
Sparse Core Ops, SparseCore 0:
  16.5 82.6 all-gather.4
  101.9 70.0 all-gather.6
  175.5 308.4 all-reduce.1
  489.2 101.0 all-gather.8
  592.9 70.8 all-gather.10
where the time goes:
time: 678 us
  waiting for transfers between devices  608 us (90%)
  local copies, waits for them, and re-layouts  31.1 us (5%)
  matrix products  15.8 us (2%)
  between operations  13.2 us (2%)
  other arithmetic  9.59 us (1%)
    psum x1, waiting for transfers between devices, shards(): density = lax.psum(partial_rows, 'band') * (1.0 / NB)  312 us
    all_gather x1, waiting for transfers between devices, shards(): lax.all_gather(kernel_part.astype(jnp.bfloat16), 'band', axis=1, tiled=True)  101 us
    all_gather x1, waiting for transfers between devices, shards(): lax.all_gather(coeffs, 'grid', axis=0, tiled=True)  71.2 us
    all_gather x1, waiting for transfers between devices, shards(): gathered = lax.all_gather(packed, 'grid', axis=0, tiled=True)  66.4 us
    all_gather x1, waiting for transfers between devices, shards(): lax.all_gather(metric, 'grid', axis=0, tiled=True)  56.5 us
    scatter x1, local copies, waits for them, and re-layouts, shards(): placing = jnp.zeros((point_count,), jnp.int32).at[by_owner].set(jnp.arang...  15.5 us
  transfers between devices with their start and end apart: 5, of which 5 were waited for; matrix products, arithmetic and copies ran while one was open for 5% of the time, Pallas kernels for 0%

commit v1 on v0

v1 whole, which is shorter than its diff:
```python
import jax
import jax.numpy as jnp
from jax import lax
from jax.sharding import PartitionSpec as P

NB = 4096
Y, Z, CORE = 2, 8, 2


def grid_index(y, z, core):
    return (y * Z + z) * CORE + core


Z_GROUPS = [[grid_index(y, z, c) for z in range(Z)] for y in range(Y) for c in range(CORE)]
YC_GROUPS = [[grid_index(y, z, c) for y in range(Y) for c in range(CORE)] for z in range(Z)]


def spread(x, count):
    return jnp.broadcast_to(x[None], (count, *x.shape))


def gather_grid(x):
    along_z = lax.all_to_all(spread(x, Z), "grid", 0, 0, axis_index_groups=Z_GROUPS, tiled=True)
    groups = lax.all_to_all(spread(along_z, Y * CORE), "grid", 0, 0, axis_index_groups=YC_GROUPS, tiled=True)
    return groups.reshape(Y * CORE * Z, *x.shape)


def exchange_band(blocks):
    return lax.all_to_all(blocks, "band", 0, 0, tiled=True)


def in_gather_order(block):
    return (block // (Z * CORE) * CORE + block % CORE) * Z + block // CORE % Z


def blocks_in_gather_order(blocks):
    shape = blocks.shape
    return blocks.reshape(Y, Z, CORE, *shape[1:]).swapaxes(1, 2).reshape(shape)


def shards(orbitals, points, theta, metric):
    row_count = orbitals.shape[0]
    point_count = points.shape[0]
    grid_count, band_count = lax.axis_size("grid"), lax.axis_size("band")
    me = lax.axis_index("grid")
    own = point_count // grid_count
    slots = jnp.arange(point_count, dtype=jnp.int32)
    by_owner, order = lax.sort_key_val(points, slots)
    my_rows = lax.dynamic_slice_in_dim(by_owner, me * own, own, 0) - me * row_count
    packed = jnp.take(orbitals, my_rows, axis=0, mode="clip")
    gathered = gather_grid(packed).reshape(point_count, -1)
    placing = lax.sort_key_val(order, slots)[1]
    placing = in_gather_order(placing // own) * own + placing % own
    sampled = jnp.take(gathered, placing, axis=0, mode="clip")
    sampled = sampled.reshape(grid_count, own, -1)

    mine = in_gather_order(me)
    my_points = lax.dynamic_index_in_dim(sampled, mine, 0, keepdims=False)
    partial_rows = lax.dot_general(
        blocks_in_gather_order(sampled), my_points, (((2,), (1,)), ((), ())), preferred_element_type=jnp.float32
    )
    density = jnp.sum(exchange_band(partial_rows), axis=0) * (1.0 / NB)
    squared = exchange_band(spread(density * density, band_count))

    metric_rows = exchange_band(spread(metric, band_count))
    product = lax.dot_general(
        metric_rows,
        sampled.astype(jnp.float32),
        (((0, 2), (0, 1)), ((), ())),
        precision=lax.Precision.HIGH,
        preferred_element_type=jnp.float32,
    )
    coeffs = lax.dot_general(
        squared,
        gather_grid(product),
        (((0, 1), (0, 1)), ((), ())),
        precision=lax.Precision.HIGH,
        preferred_element_type=jnp.float32,
    ).astype(jnp.bfloat16)
    coeffs = gather_grid(coeffs).reshape(point_count, -1)
    return jnp.dot(theta, coeffs, preferred_element_type=jnp.float32).astype(jnp.bfloat16)


def solution(mesh):
    placed = (P("grid", "band"), P(), P("grid", None), P("grid", "band"))
    return jax.shard_map(
        shards, mesh=mesh, in_specs=placed, out_specs=P("grid", "band"), check_vma=False
    )
```

time: 678 us -> 344 us (0.51)
  waiting for transfers between devices: 608 us -> 73.5 us
  blocking collectives: 0 us -> 197 us
  starting transfers between devices: 0.17 us -> 28.1 us
  between operations: 13.2 us -> 0.19 us
  local copies, waits for them, and re-layouts: 31.1 us -> 19.7 us
    psum x1 -> x0, waiting for transfers between devices: 312 us -> none  [shards(): density = lax.psum(partial_rows, 'band') * (1.0 / NB)]
    all_gather x4 -> x0, waiting for transfers between devices: 295 us -> none  [the longest x1 101 us: shards(): lax.all_gather(kernel_part.astype(jnp.bfloat16), 'band', axis=1, tiled=True)]
    all_to_all x0 -> x6, blocking collectives: none -> 197 us  [the longest x2 120 us: exchange_band(): return lax.all_to_all(blocks, 'band', 0, 0, tiled=True)]
    all_to_all x0 -> x3, waiting for transfers between devices: none -> 73.5 us  [the longest x1 39.2 us: exchange_band(): return lax.all_to_all(blocks, 'band', 0, 0, tiled=True)]
    all_to_all x0 -> x3, starting transfers between devices: none -> 28.1 us  [the longest x1 12.4 us: exchange_band(): return lax.all_to_all(blocks, 'band', 0, 0, tiled=True)]
    scatter x1 -> x0, local copies, waits for them, and re-layouts: 15.5 us -> none  [shards(): placing = jnp.zeros((point_count,), jnp.int32).at[by_owner].set(jnp.arang...]
    gather x3 -> x2, local copies, waits for them, and re-layouts: 14.7 us -> 12.8 us  [the longest x1 12.1 us: shards(): sampled = jnp.take(gathered, placing, axis=0, mode='clip')]
  transfers between devices with their start and end apart: 5 -> 3, of which waited for: 5 -> 3; matrix products, arithmetic and copies ran while one was open for 5% -> 6% of each run, Pallas kernels for 0% -> 0%
where the time goes in v1:
time: 344 us; the launch traced here: 343 us
  blocking collectives  197 us (57%)
  waiting for transfers between devices  73.5 us (21%)
  starting transfers between devices  28.1 us (8%)
  local copies, waits for them, and re-layouts  19.7 us (6%)
  other arithmetic  13.6 us (4%)
  matrix products  10.5 us (3%)
    all_to_all x2, blocking collectives, exchange_band(): return lax.all_to_all(blocks, 'band', 0, 0, tiled=True)  120 us
    all_to_all x2, blocking collectives, gather_grid(): lax.all_to_all(spread(x, Z), 'grid', 0, 0, axis_index_groups=Z_GROUPS, ti...  39.8 us
    all_to_all x1, waiting for transfers between devices, exchange_band(): return lax.all_to_all(blocks, 'band', 0, 0, tiled=True)  39.2 us
    all_to_all x2, blocking collectives, gather_grid(): lax.all_to_all(spread(along_z, Y * CORE), 'grid', 0, 0, axis_index_groups...  37.3 us
    all_to_all x1, waiting for transfers between devices, gather_grid(): lax.all_to_all(spread(along_z, Y * CORE), 'grid', 0, 0, axis_index_groups...  22.6 us
    all_to_all x1, starting transfers between devices, exchange_band(): return lax.all_to_all(blocks, 'band', 0, 0, tiled=True)  12.4 us
    gather x1, local copies, waits for them, and re-layouts, shards(): sampled = jnp.take(gathered, placing, axis=0, mode='clip')  12.1 us
    all_to_all x1, waiting for transfers between devices, gather_grid(): lax.all_to_all(spread(x, Z), 'grid', 0, 0, axis_index_groups=Z_GROUPS, ti...  11.7 us
  transfers between devices with their start and end apart: 3, of which 3 were waited for; matrix products, arithmetic and copies ran while one was open for 6% of the time, Pallas kernels for 0%

profile of v1, /device:TPU:1, one launch (start us, length us, event | category | flops | bytes accessed | tf_op | source)
XLA Modules:
  0.0 342.7 jit_solution(1540309879554051006)
XLA Ops:
  0.0 0.0 copy-start
  0.0 5.9 %sort.30 = (s32[4096]{0:T(1024)S(1)}, s32[4096]{0:T(1024)S(1)}) sort(s32[4096]{0:T(1024)} %param.5, s32[4096]{0:T(1024)S(1)} %iota.5), dimensions={0}, to_apply=%region_0.0 | sort | flops 49152 | bytes 65536 | tf_op jit(solution)/shard_map/sort | solution.py:48
  5.9 0.1 dynamic-slice_subtract_fusion
  6.0 0.0 copy-done
  6.0 0.7 gather_fusion
  6.8 0.0 copy-start.1
  6.8 27.5 %all_to_all.45 = bf16[8,128,128]{2,1,0:T(8,128)(2,1)S(1)} all-to-all(bf16[8,128,128]{2,1,0:T(8,128)(2,1)S(1)} %broadcast_in_dim.25), channel_id=1, replica_groups={{0,64,128,192,256,320,384,448},{32,96,160,224,288,352,416,480},{512,576..., dimensions={0} | all-to-all | bytes 524288 | tf_op jit(solution)/shard_map/all_to_all | solution.py:23
  34.3 0.2 broadcast_in_dim.26
  34.5 18.5 %all_to_all.46 = bf16[4,8,128,128]{3,2,1,0:T(8,128)(2,1)S(1)} all-to-all(bf16[4,8,128,128]{3,2,1,0:T(8,128)(2,1)S(1)} %broadcast_in_dim.26), channel_id=1, replica_groups={{0,32,512,544},{64,96,576,608},{128,160,640,672},{192,224,704,736},{256..., dimensions={0} | all-to-all | bytes 2097152 | tf_op jit(solution)/shard_map/all_to_all | solution.py:24
  53.0 0.0 copy-done.1
  53.0 1.5 broadcast_in_dim.29
  54.6 12.4 %all-to-all-start.4 = ((f32[32,128,128]{2,1,0:T(8,128)}), f32[32,128,128]{2,1,0:T(8,128)}, u32[]{:S(2)}, u32[]{:S(2)}) async-start(f32[32,128,128]{2,1,0:T(8,128)} %broadcast_in_dim.29), calls=%async_computation.4 | async-start | bytes 4194304 | tf_op jit(solution)/shard_map/all_to_all | solution.py:29
  67.0 5.8 %sort.31 = (s32[4096]{0:T(1024)}, s32[4096]{0:T(1024)S(1)}) sort(s32[4096]{0:T(1024)S(1)} %get-tuple-element.9, s32[4096]{0:T(1024)S(1)} %iota.6), dimensions={0}, to_apply=%region_1.2 | sort | flops 49152 | bytes 65536 | tf_op jit(solution)/shard_map/sort | solution.py:52
  72.7 0.1 fusion.12
  72.8 12.1 %gather_fusion.1 = bf16[4096,128]{1,0:T(8,128)(2,1)S(1)} fusion(bf16[4096,128]{1,0:T(8,128)(2,1)S(1)} %bitcast.29, s32[4096]{0:T(1024)S(1)} %fusion.12), kind=kCustom, calls=%fused_computation.1 | custom fusion | bytes 2113536 | tf_op jit(solution)/shard_map/jit(_take)/gather | solution.py:54
  84.9 39.2 %all-to-all-done.4 = f32[32,128,128]{2,1,0:T(8,128)} async-done(((f32[32,128,128]{2,1,0:T(8,128)}), f32[32,128,128]{2,1,0:T(8,128)}, u32[]{:S(2)}, u32[]{:S(2)}) %all-to-all-start.4) | async-done | bytes 2097184 | tf_op jit(solution)/shard_map/all_to_all | solution.py:29
  124.2 2.5 convolution_bitcast_fusion.1
  126.7 0.1 copy.15
  126.8 0.8 broadcast_in_dim.30
  127.6 4.2 %all-to-all-start.5 = ((f32[8,128,128]{2,1,0:T(8,128)}), f32[8,128,128]{2,1,0:T(8,128)}, u32[]{:S(2)}, u32[]{:S(2)}) async-start(f32[8,128,128]{2,1,0:T(8,128)} %broadcast_in_dim.30), calls=%async_computation.5 | async-start | bytes 1048576 | tf_op jit(solution)/shard_map/all_to_all | solution.py:23
  131.8 0.1 copy.12
  132.0 0.4 fusion.2
  132.4 11.7 %all-to-all-done.5 = f32[8,128,128]{2,1,0:T(8,128)} async-done(((f32[8,128,128]{2,1,0:T(8,128)}), f32[8,128,128]{2,1,0:T(8,128)}, u32[]{:S(2)}, u32[]{:S(2)}) %all-to-all-start.5) | async-done | bytes 524320 | tf_op jit(solution)/shard_map/all_to_all | solution.py:23
  144.1 63.1 %all_to_all.47 = f32[32,128,128]{2,1,0:T(8,128)} all-to-all(f32[32,128,128]{2,1,0:T(8,128)S(1)} %fusion.2), channel_id=1, replica_groups=mesh['grid'=32,'band'=32] {'band'}, dimensions={0} | all-to-all | bytes 4194304 | tf_op jit(solution)/shard_map/all_to_all | solution.py:29
  207.2 2.6 broadcast_in_dim.31
  209.8 11.6 %all-to-all-start.6 = ((f32[4,8,128,128]{3,2,1,0:T(8,128)}), f32[4,8,128,128]{3,2,1,0:T(8,128)S(1)}, u32[]{:S(2)}, u32[]{:S(2)}) async-start(f32[4,8,128,128]{3,2,1,0:T(8,128)} %broadcast_in_dim.31), calls=%async_computation.6 | async-start | bytes 4194304 | tf_op jit(solution)/shard_map/all_to_all | solution.py:24
  221.4 1.7 reduce_sum.9
  223.1 0.1 copy.13
  223.2 22.6 %all-to-all-done.6 = f32[4,8,128,128]{3,2,1,0:T(8,128)S(1)} async-done(((f32[4,8,128,128]{3,2,1,0:T(8,128)}), f32[4,8,128,128]{3,2,1,0:T(8,128)S(1)}, u32[]{:S(2)}, u32[]{:S(2)}) %all-to-all-start.6) | async-done | bytes 2097184 | tf_op jit(solution)/shard_map/all_to_all | solution.py:24
  245.8 0.2 broadcast_in_dim.28
  246.1 57.0 %all_to_all.48 = f32[32,128,128]{1,2,0:T(8,128)S(1)} all-to-all(f32[32,128,128]{1,2,0:T(8,128)S(1)} %broadcast_in_dim.28), channel_id=1, replica_groups=mesh['grid'=32,'band'=32] {'band'}, dimensions={0} | all-to-all | bytes 4194304 | tf_op jit(solution)/shard_map/all_to_all | solution.py:29
  303.0 1.2 fusion.1
  304.3 12.3 %all_to_all.49 = bf16[8,128,128]{2,1,0:T(8,128)(2,1)S(1)} all-to-all(bf16[8,128,128]{2,1,0:T(8,128)(2,1)S(1)} %broadcast_in_dim.32), channel_id=1, replica_groups={{0,64,128,192,256,320,384,448},{32,96,160,224,288,352,416,480},{512,576..., dimensions={0} | all-to-all | bytes 524288 | tf_op jit(solution)/shard_map/all_to_all | solution.py:23
  316.6 0.2 broadcast_in_dim.33
  316.8 18.8 %all_to_all.50 = bf16[4,8,128,128]{3,2,1,0:T(8,128)(2,1)S(1)} all-to-all(bf16[4,8,128,128]{3,2,1,0:T(8,128)(2,1)S(1)} %broadcast_in_dim.33), channel_id=1, replica_groups={{0,32,512,544},{64,96,576,608},{128,160,640,672},{192,224,704,736},{256..., dimensions={0} | all-to-all | bytes 2097152 | tf_op jit(solution)/shard_map/all_to_all | solution.py:24
  335.6 6.3 %fusion = bf16[1024,128]{0,1:T(8,128)(2,1)S(1)} fusion(bf16[4096,128]{1,0:T(8,128)(2,1)S(1)} %bitcast.34, bf16[1024,4096]{1,0:T(8,128)(2,1)} %param.6), kind=kOutput, calls=%fused_computation.3 | convolution fusion | flops 1073872896 | bytes 9699328 | tf_op jit(solution)/shard_map/dot_general | solution.py:81
  341.9 0.8 copy.16
  (6 shorter events, 0.1 us)
Async XLA Ops:
  0.0 6.0 %copy-start = (bf16[1024,128]{1,0:T(8,128)(2,1)S(1)}, bf16[1024,128]{1,0:T(8,128)(2,1)}, u32[]{:S(2)}) copy-start(bf16[1024,128]{1,0:T(8,128)(2,1)} %param.4) | copy-start | bytes 786436
  6.8 46.3 %copy-start.1 = (f32[128,128]{1,0:T(8,128)S(1)}, f32[128,128]{1,0:T(8,128)}, u32[]{:S(2)}) copy-start(f32[128,128]{1,0:T(8,128)} %param.7) | copy-start | bytes 196612
  54.6 69.6 %all-to-all-start.4 = ((f32[32,128,128]{2,1,0:T(8,128)}), f32[32,128,128]{2,1,0:T(8,128)}, u32[]{:S(2)}, u32[]{:S(2)}) async-start(f32[32,128,128]{2,1,0:T(8,128)} %broadcast_in_dim.29), calls=%async_computation.4 | async-start | bytes 4194304 | tf_op jit(solution)/shard_map/all_to_all | solution.py:29
  127.6 16.5 %all-to-all-start.5 = ((f32[8,128,128]{2,1,0:T(8,128)}), f32[8,128,128]{2,1,0:T(8,128)}, u32[]{:S(2)}, u32[]{:S(2)}) async-start(f32[8,128,128]{2,1,0:T(8,128)} %broadcast_in_dim.30), calls=%async_computation.5 | async-start | bytes 1048576 | tf_op jit(solution)/shard_map/all_to_all | solution.py:23
  209.8 36.0 %all-to-all-start.6 = ((f32[4,8,128,128]{3,2,1,0:T(8,128)}), f32[4,8,128,128]{3,2,1,0:T(8,128)S(1)}, u32[]{:S(2)}, u32[]{:S(2)}) async-start(f32[4,8,128,128]{3,2,1,0:T(8,128)} %broadcast_in_dim.31), calls=%async_computation.6 | async-start | bytes 4194304 | tf_op jit(solution)/shard_map/all_to_all | solution.py:24

commit v2 on v1

v2 whole, which is shorter than its diff:
```python
import jax
import jax.numpy as jnp
from jax import lax
from jax.sharding import PartitionSpec as P

NB = 4096
Y, Z, CORE = 2, 8, 2


def grid_index(y, z, core):
    return (y * Z + z) * CORE + core


Z_GROUPS = [[grid_index(y, z, c) for z in range(Z)] for y in range(Y) for c in range(CORE)]
YC_GROUPS = [[grid_index(y, z, c) for y in range(Y) for c in range(CORE)] for z in range(Z)]
GRID_BITS = (8, 4, 2, 16, 1)
BAND_BITS = (16, 8, 4, 2, 1)


def spread(x, count):
    return jnp.broadcast_to(x[None], (count, *x.shape))


def gather_z(x):
    return lax.all_to_all(spread(x, Z), "grid", 0, 0, axis_index_groups=Z_GROUPS, tiled=True)


def gather_yc(along_z):
    groups = lax.all_to_all(spread(along_z, Y * CORE), "grid", 0, 0, axis_index_groups=YC_GROUPS, tiled=True)
    return groups.reshape(Y * CORE * Z, *along_z.shape[1:])


def exchange_band(blocks):
    return lax.all_to_all(blocks, "band", 0, 0, tiled=True)


def gather_doubling(x, axis, bits):
    count = lax.axis_size(axis)
    x = x[None]
    for bit in bits:
        x = jnp.concatenate([x, lax.ppermute(x, axis, [(j, j ^ bit) for j in range(count)])])
    return x


def doubled_place(k, bits):
    return sum((k // bit % 2) << i for i, bit in enumerate(bits))


def in_gather_order(block):
    return (block // (Z * CORE) * CORE + block % CORE) * Z + block // CORE % Z


def take(rows, index):
    return jnp.take(rows, index, axis=0, mode="clip")


def shards(orbitals, points, theta, metric):
    row_count = orbitals.shape[0]
    point_count = points.shape[0]
    grid_count, band_count = lax.axis_size("grid"), lax.axis_size("band")
    me = lax.axis_index("grid")
    own = point_count // grid_count
    slots = jnp.arange(point_count, dtype=jnp.int32)
    by_owner, order = lax.sort_key_val(points, slots)
    my_rows = lax.dynamic_slice_in_dim(by_owner, me * own, own, 0) - me * row_count
    packed = take(orbitals, my_rows)
    along_z = gather_z(packed)
    metric_rows = gather_doubling(metric.astype(jnp.bfloat16), "band", BAND_BITS)
    gathered = gather_yc(along_z).reshape(point_count, -1)
    placing = lax.sort_key_val(order, slots)[1]
    placing = in_gather_order(placing // own) * own + placing % own

    mine = in_gather_order(me)
    my_points = take(gathered, lax.dynamic_slice_in_dim(placing, mine * own, own, 0))
    partial_rows = lax.dot_general(
        gathered, my_points, (((1,), (1,)), ((), ())), preferred_element_type=jnp.float32
    ).astype(jnp.bfloat16)
    partial_rows = exchange_band(partial_rows.reshape(grid_count, own, own))
    blocks = [0] * band_count
    for k in range(band_count):
        blocks[doubled_place(k, BAND_BITS)] = k
    blocks = jnp.asarray(blocks, jnp.int32) ^ lax.axis_index("band")
    sampled = take(gathered, take(placing.reshape(band_count, own), blocks).reshape(point_count))
    product = lax.dot_general(
        metric_rows,
        sampled.reshape(grid_count, own, -1),
        (((0, 2), (0, 1)), ((), ())),
        preferred_element_type=jnp.float32,
    ).astype(jnp.bfloat16)
    products = gather_doubling(product, "grid", GRID_BITS).reshape(point_count, -1)
    density = jnp.sum(partial_rows.astype(jnp.float32), axis=0) * (1.0 / NB)
    squared = (density * density).astype(jnp.bfloat16)
    squared = exchange_band(spread(squared, band_count))
    order = order.reshape(Y, Z, CORE, own).swapaxes(1, 2).reshape(point_count)
    products = take(products, doubled_place(order // own ^ me, GRID_BITS) * own + order % own)
    coeffs = lax.dot_general(
        squared,
        products.reshape(grid_count, own, -1),
        (((0, 1), (0, 1)), ((), ())),
        preferred_element_type=jnp.float32,
    ).astype(jnp.bfloat16)
    coeffs = gather_yc(gather_z(coeffs)).reshape(point_count, -1)
    return jnp.dot(theta, coeffs, preferred_element_type=jnp.float32).astype(jnp.bfloat16)


def solution(mesh):
    placed = (P("grid", "band"), P(), P("grid", None), P("grid", "band"))
    return jax.shard_map(
        shards, mesh=mesh, in_specs=placed, out_specs=P("grid", "band"), check_vma=False
    )
```

time: 344 us -> 268 us (0.78)
  blocking collectives: 197 us -> 59.7 us
  starting transfers between devices: 28.1 us -> 60.7 us
  local copies, waits for them, and re-layouts: 19.7 us -> 37.2 us
  waiting for transfers between devices: 73.5 us -> 83.4 us
    all_to_all x6 -> x3, blocking collectives: 197 us -> 59.7 us  [the longest x2 42.1 us: gather_z(): lax.all_to_all(spread(x, Z), 'grid', 0, 0, axis_index_groups=Z_GROUPS, ti...]
    ppermute x0 -> x10, waiting for transfers between devices: none -> 83.4 us  [gather_doubling(): lax.ppermute(x, axis, [(j, j ^ bit) for j in range(count)])]
    all_to_all x1 -> x2, waiting for transfers between devices: 39.2 us -> 0.01 us  [exchange_band(): return lax.all_to_all(blocks, 'band', 0, 0, tiled=True)]
    all_to_all x2 -> x1, waiting for transfers between devices: 34.3 us -> 0.01 us  [gather_yc(): lax.all_to_all(spread(along_z, Y * CORE), 'grid', 0, 0, axis_index_groups...]
    ppermute x0 -> x10, starting transfers between devices: none -> 32.5 us  [gather_doubling(): lax.ppermute(x, axis, [(j, j ^ bit) for j in range(count)])]
    gather x2 -> x5, local copies, waits for them, and re-layouts: 12.8 us -> 26.3 us  [take(): return jnp.take(rows, index, axis=0, mode='clip')]
    all_to_all x1 -> x2, starting transfers between devices: 12.4 us -> 22.4 us  [exchange_band(): return lax.all_to_all(blocks, 'band', 0, 0, tiled=True)]
    all_to_all x2 -> x1, starting transfers between devices: 15.8 us -> 5.82 us  [gather_yc(): lax.all_to_all(spread(along_z, Y * CORE), 'grid', 0, 0, axis_index_groups...]
  transfers between devices with their start and end apart: 3 -> 13, of which waited for: 3 -> 8; matrix products, arithmetic and copies ran while one was open for 6% -> 17% of each run, Pallas kernels for 0% -> 0%
where the time goes in v2:
time: 268 us; the launch traced here: 267 us
  waiting for transfers between devices  83.4 us (31%)
  starting transfers between devices  60.7 us (23%)
  blocking collectives  59.7 us (22%)
  local copies, waits for them, and re-layouts  37.2 us (14%)
  other arithmetic  14.9 us (6%)
  matrix products  10.4 us (4%)
    ppermute x10, waiting for transfers between devices, gather_doubling(): lax.ppermute(x, axis, [(j, j ^ bit) for j in range(count)])  83.4 us
    all_to_all x2, blocking collectives, gather_z(): lax.all_to_all(spread(x, Z), 'grid', 0, 0, axis_index_groups=Z_GROUPS, ti...  42.1 us
    ppermute x10, starting transfers between devices, gather_doubling(): lax.ppermute(x, axis, [(j, j ^ bit) for j in range(count)])  32.5 us
    gather x5, local copies, waits for them, and re-layouts, take(): return jnp.take(rows, index, axis=0, mode='clip')  26.3 us
    all_to_all x2, starting transfers between devices, exchange_band(): return lax.all_to_all(blocks, 'band', 0, 0, tiled=True)  22.4 us
    all_to_all x1, blocking collectives, gather_yc(): lax.all_to_all(spread(along_z, Y * CORE), 'grid', 0, 0, axis_index_groups...  17.5 us
    dot_general x1, matrix products, shards(): jnp.dot(theta, coeffs, preferred_element_type=jnp.float32)  6.3 us
    sort x1, other arithmetic, shards(): by_owner, order = lax.sort_key_val(points, slots)  5.93 us
  transfers between devices with their start and end apart: 13, of which 8 were waited for; matrix products, arithmetic and copies ran while one was open for 17% of the time, Pallas kernels for 0%

profile of v2, /device:TPU:1, one launch (start us, length us, event | category | flops | bytes accessed | tf_op | source)
XLA Modules:
  0.0 266.6 jit_solution(18315587741876485828)
XLA Ops:
  0.0 5.9 %sort.30 = (s32[4096]{0:T(1024)S(1)}, s32[4096]{0:T(1024)S(1)}) sort(s32[4096]{0:T(1024)} %param.6, s32[4096]{0:T(1024)S(1)} %iota.5), dimensions={0}, to_apply=%region_0.0 | sort | flops 49152 | bytes 65536 | tf_op jit(solution)/shard_map/sort | solution.py:64
  5.9 0.7 broadcast_xor_fusion
  6.7 0.7 gather_fusion
  7.4 27.5 %all_to_all.30 = bf16[8,128,128]{2,1,0:T(8,128)(2,1)S(1)} all-to-all(bf16[8,128,128]{2,1,0:T(8,128)(2,1)S(1)} %broadcast_in_dim.54), channel_id=1, replica_groups={{0,64,128,192,256,320,384,448},{32,96,160,224,288,352,416,480},{512,576..., dimensions={0} | all-to-all | bytes 524288 | tf_op jit(solution)/shard_map/all_to_all | solution.py:25
  35.0 1.2 broadcast_in_dim.55
  36.2 5.8 %all-to-all-start.1 = ((bf16[4,8,128,128]{3,2,1,0:T(8,128)(2,1)}), bf16[4,8,128,128]{3,2,1,0:T(8,128)(2,1)S(1)}, u32[]{:S(2)}, u32[]{:S(2)}) async-start(bf16[4,8,128,128]{3,2,1,0:T(8,128)(2,1)} %broadcast_in_dim.55), calls=%async_computation.1 | async-start | bytes 2097152 | tf_op jit(solution)/shard_map/all_to_all | solution.py:29
  42.0 1.5 constant_dynamic-update-slice_fusion.4
  43.4 7.9 %collective-permute-start = (bf16[1,128,128]{2,1,0:T(8,128)(2,1)S(1)}, bf16[1,128,128]{2,1,0:T(8,128)(2,1)S(1)}, u32[]{:S(2)}, u32[]{:S(2)}) collective-permute-start(bf16[1,128,128]{2,1,0:T(8,128)(2,1)S(1)} %get-tuple-element.12), channel_id=1, source_target_pairs={{0,16},{1,17},{2,18},{3,19},{4,20},{5,21},{6,22},{7,23},{8,24},{9,... | collective-permute-start | bytes 98312 | tf_op jit(solution)/shard_map/ppermute | solution.py:41
  51.4 5.8 %sort.31 = (s32[4096]{0:T(1024)}, s32[4096]{0:T(1024)S(1)}) sort(s32[4096]{0:T(1024)S(1)} %get-tuple-element.9, s32[4096]{0:T(1024)S(1)} %iota.6), dimensions={0}, to_apply=%region_1.2 | sort | flops 49152 | bytes 65536 | tf_op jit(solution)/shard_map/sort | solution.py:70
  57.3 0.7 gather_fusion.1
  58.0 1.4 convolution_convert_fusion
  59.4 10.7 %all-to-all-start.2 = ((bf16[32,128,128]{2,1,0:T(8,128)(2,1)}), bf16[32,128,128]{2,1,0:T(8,128)(2,1)S(1)}, u32[]{:S(2)}, u32[]{:S(2)}) async-start(bf16[32,128,128]{2,1,0:T(8,128)(2,1)} %bitcast.1), calls=%async_computation.2 | async-start | bytes 2097152 | tf_op jit(solution)/shard_map/all_to_all | solution.py:34
  70.2 4.0 %collective-permute-start.1 = (bf16[2,128,128]{2,1,0:T(8,128)(2,1)S(1)}, bf16[2,128,128]{2,1,0:T(8,128)(2,1)S(1)}, u32[]{:S(2)}, u32[]{:S(2)}) collective-permute-start(bf16[2,128,128]{2,1,0:T(8,128)(2,1)S(1)} %pad_maximum_fusion.4), channel_id=1, source_target_pairs={{0,8},{1,9},{2,10},{3,11},{4,12},{5,13},{6,14},{7,15},{8,0},{9,1},... | collective-permute-start | bytes 196616 | tf_op jit(solution)/shard_map/ppermute | solution.py:41
  74.2 25.9 %collective-permute-done.1 = bf16[2,128,128]{2,1,0:T(8,128)(2,1)S(1)} collective-permute-done((bf16[2,128,128]{2,1,0:T(8,128)(2,1)S(1)}, bf16[2,128,128]{2,1,0:T(8,128)(2,1)S(1)}, u32[]{:S(2)}, u32[]{:S(2)}) %collective-permute-start.1) | collective-permute-done | bytes 65568 | tf_op jit(solution)/shard_map/ppermute | solution.py:41
  100.1 6.3 %collective-permute-start.2 = (bf16[4,128,128]{2,1,0:T(8,128)(2,1)S(1)}, bf16[4,128,128]{2,1,0:T(8,128)(2,1)S(1)}, u32[]{:S(2)}, u32[]{:S(2)}) collective-permute-start(bf16[4,128,128]{2,1,0:T(8,128)(2,1)S(1)} %pad_maximum_fusion.2), channel_id=1, source_target_pairs={{0,4},{1,5},{2,6},{3,7},{4,0},{5,1},{6,2},{7,3},{8,12},{9,13},{10,... | collective-permute-start | bytes 393224 | tf_op jit(solution)/shard_map/ppermute | solution.py:41
  106.4 0.6 constant_dynamic-update-slice_fusion.10
  107.0 6.0 %collective-permute-done.2 = bf16[4,128,128]{2,1,0:T(8,128)(2,1)S(1)} collective-permute-done((bf16[4,128,128]{2,1,0:T(8,128)(2,1)S(1)}, bf16[4,128,128]{2,1,0:T(8,128)(2,1)S(1)}, u32[]{:S(2)}, u32[]{:S(2)}) %collective-permute-start.2) | collective-permute-done | bytes 131104 | tf_op jit(solution)/shard_map/ppermute | solution.py:41
  113.0 1.9 collective-permute-start.3
  114.9 0.6 constant_dynamic-update-slice_fusion.3
  115.5 0.7 constant_dynamic-update-slice_fusion.2
  116.2 0.7 constant_dynamic-update-slice_fusion.1
  116.9 7.8 %collective-permute-done.3 = bf16[8,128,128]{2,1,0:T(8,128)(2,1)S(1)} collective-permute-done((bf16[8,128,128]{2,1,0:T(8,128)(2,1)S(1)}, bf16[8,128,128]{2,1,0:T(8,128)(2,1)S(1)}, u32[]{:S(2)}, u32[]{:S(2)}) %collective-permute-start.3) | collective-permute-done | bytes 262176 | tf_op jit(solution)/shard_map/ppermute | solution.py:41
  124.7 0.9 constant_dynamic-update-slice_fusion
  125.7 2.0 collective-permute-start.4
  128.3 10.4 %collective-permute-done.4 = bf16[16,128,128]{2,1,0:T(8,128)(2,1)S(1)} collective-permute-done((bf16[16,128,128]{2,1,0:T(8,128)(2,1)}, bf16[16,128,128]{2,1,0:T(8,128)(2,1)S(1)}, u32[]{:S(2)}, u32[]{:S(2)}) %collective-permute-start.4) | collective-permute-done | bytes 524320 | tf_op jit(solution)/shard_map/ppermute | solution.py:41
  138.7 0.8 constant_dynamic-update-slice_fusion.5
  139.5 12.1 %gather_fusion.3 = bf16[4096,128]{1,0:T(8,128)(2,1)S(1)} fusion(bf16[4096,128]{1,0:T(8,128)(2,1)S(1)} %bitcast.42, s32[4096]{0:T(1024)S(1)} %bitcast_clamp_fusion), kind=kCustom, calls=%fused_computation.3 | custom fusion | bytes 2113536 | tf_op jit(solution)/shard_map/jit(_take)/gather | solution.py:54
  151.6 2.3 constant_dynamic-update-slice_fusion.15
  153.9 2.1 collective-permute-start.5
  156.0 6.5 %collective-permute-done.5 = bf16[1,128,128]{2,1,0:T(8,128)(2,1)S(1)} collective-permute-done((bf16[1,128,128]{2,1,0:T(8,128)(2,1)S(1)}, bf16[1,128,128]{2,1,0:T(8,128)(2,1)S(1)}, u32[]{:S(2)}, u32[]{:S(2)}) %collective-permute-start.5) | collective-permute-done | bytes 32800 | tf_op jit(solution)/shard_map/ppermute | solution.py:41
  162.6 1.9 collective-permute-start.6
  164.8 1.2 broadcast_in_dim.57
  166.0 11.6 %all-to-all-start.3 = ((bf16[32,128,128]{1,2,0:T(8,128)(2,1)}), bf16[32,128,128]{1,2,0:T(8,128)(2,1)S(1)}, u32[]{:S(2)}, u32[]{:S(2)}) async-start(bf16[32,128,128]{1,2,0:T(8,128)(2,1)} %broadcast_in_dim.57), calls=%async_computation.3 | async-start | bytes 2097152 | tf_op jit(solution)/shard_map/all_to_all | solution.py:34
  177.7 2.1 collective-permute-start.7
  179.8 3.6 %collective-permute-done.7 = bf16[4,128,128]{2,1,0:T(8,128)(2,1)S(1)} collective-permute-done((bf16[4,128,128]{2,1,0:T(8,128)(2,1)S(1)}, bf16[4,128,128]{2,1,0:T(8,128)(2,1)S(1)}, u32[]{:S(2)}, u32[]{:S(2)}) %collective-permute-start.7) | collective-permute-done | bytes 131104 | tf_op jit(solution)/shard_map/ppermute | solution.py:41
  183.4 1.9 collective-permute-start.8
  186.0 0.6 constant_dynamic-update-slice_fusion.13
  186.6 0.7 constant_dynamic-update-slice_fusion.12
  187.3 22.2 %collective-permute-done.8 = bf16[8,128,128]{2,1,0:T(8,128)(2,1)S(1)} collective-permute-done((bf16[8,128,128]{2,1,0:T(8,128)(2,1)S(1)}, bf16[8,128,128]{2,1,0:T(8,128)(2,1)S(1)}, u32[]{:S(2)}, u32[]{:S(2)}) %collective-permute-start.8) | collective-permute-done | bytes 262176 | tf_op jit(solution)/shard_map/ppermute | solution.py:41
  209.5 0.8 constant_dynamic-update-slice_fusion.11
  210.3 2.3 collective-permute-start.9
  212.6 0.6 fusion.4
  213.3 1.1 collective-permute-done.9
  214.4 12.1 %gather_fusion.4 = bf16[4096,128]{1,0:T(8,128)(2,1)S(1)} fusion(bf16[4096,128]{1,0:T(8,128)(2,1)S(1)} %bitcast.43, s32[4096]{0:T(1024)S(1)} %broadcast_clamp_fusion), kind=kCustom, calls=%fused_computation.4 | custom fusion | bytes 2113536 | tf_op jit(solution)/shard_map/jit(_take)/gather | solution.py:54
  227.1 14.6 %all_to_all.31 = bf16[8,128,128]{2,1,0:T(8,128)(2,1)S(1)} all-to-all(bf16[8,128,128]{2,1,0:T(8,128)(2,1)S(1)} %broadcast_in_dim.62), channel_id=1, replica_groups={{0,64,128,192,256,320,384,448},{32,96,160,224,288,352,416,480},{512,576..., dimensions={0} | all-to-all | bytes 524288 | tf_op jit(solution)/shard_map/all_to_all | solution.py:25
  241.9 17.5 %all_to_all.32 = bf16[4,8,128,128]{3,2,1,0:T(8,128)(2,1)S(1)} all-to-all(bf16[4,8,128,128]{3,2,1,0:T(8,128)(2,1)S(1)} %broadcast_in_dim.63), channel_id=1, replica_groups={{0,32,512,544},{64,96,576,608},{128,160,640,672},{192,224,704,736},{256..., dimensions={0} | all-to-all | bytes 2097152 | tf_op jit(solution)/shard_map/all_to_all | solution.py:29
  259.4 6.3 %fusion = bf16[1024,128]{0,1:T(8,128)(2,1)S(1)} fusion(bf16[4096,128]{1,0:T(8,128)(2,1)S(1)} %bitcast.46, bf16[1024,4096]{1,0:T(8,128)(2,1)} %param.7), kind=kOutput, calls=%fused_computation.8 | convolution fusion | flops 1073872896 | bytes 9699328 | tf_op jit(solution)/shard_map/dot_general | solution.py:103
  265.7 0.8 copy.12
  (34 shorter events, 2.7 us)
Async XLA Ops:
  0.0 6.7 %copy-start = (bf16[1024,128]{1,0:T(8,128)(2,1)S(1)}, bf16[1024,128]{1,0:T(8,128)(2,1)}, u32[]{:S(2)}) copy-start(bf16[1024,128]{1,0:T(8,128)(2,1)} %param.5) | copy-start | bytes 786436
  36.2 21.2 %all-to-all-start.1 = ((bf16[4,8,128,128]{3,2,1,0:T(8,128)(2,1)}), bf16[4,8,128,128]{3,2,1,0:T(8,128)(2,1)S(1)}, u32[]{:S(2)}, u32[]{:S(2)}) async-start(bf16[4,8,128,128]{3,2,1,0:T(8,128)(2,1)} %broadcast_in_dim.55), calls=%async_computation.1 | async-start | bytes 2097152 | tf_op jit(solution)/shard_map/all_to_all | solution.py:29
  43.4 26.7 %collective-permute-start = (bf16[1,128,128]{2,1,0:T(8,128)(2,1)S(1)}, bf16[1,128,128]{2,1,0:T(8,128)(2,1)S(1)}, u32[]{:S(2)}, u32[]{:S(2)}) collective-permute-start(bf16[1,128,128]{2,1,0:T(8,128)(2,1)S(1)} %get-tuple-element.12), channel_id=1, source_target_pairs={{0,16},{1,17},{2,18},{3,19},{4,20},{5,21},{6,22},{7,23},{8,24},{9,... | collective-permute-start | bytes 98312 | tf_op jit(solution)/shard_map/ppermute | solution.py:41
  59.4 105.1 %all-to-all-start.2 = ((bf16[32,128,128]{2,1,0:T(8,128)(2,1)}), bf16[32,128,128]{2,1,0:T(8,128)(2,1)S(1)}, u32[]{:S(2)}, u32[]{:S(2)}) async-start(bf16[32,128,128]{2,1,0:T(8,128)(2,1)} %bitcast.1), calls=%async_computation.2 | async-start | bytes 2097152 | tf_op jit(solution)/shard_map/all_to_all | solution.py:34
  70.2 29.9 %collective-permute-start.1 = (bf16[2,128,128]{2,1,0:T(8,128)(2,1)S(1)}, bf16[2,128,128]{2,1,0:T(8,128)(2,1)S(1)}, u32[]{:S(2)}, u32[]{:S(2)}) collective-permute-start(bf16[2,128,128]{2,1,0:T(8,128)(2,1)S(1)} %pad_maximum_fusion.4), channel_id=1, source_target_pairs={{0,8},{1,9},{2,10},{3,11},{4,12},{5,13},{6,14},{7,15},{8,0},{9,1},... | collective-permute-start | bytes 196616 | tf_op jit(solution)/shard_map/ppermute | solution.py:41
  100.1 12.9 %collective-permute-start.2 = (bf16[4,128,128]{2,1,0:T(8,128)(2,1)S(1)}, bf16[4,128,128]{2,1,0:T(8,128)(2,1)S(1)}, u32[]{:S(2)}, u32[]{:S(2)}) collective-permute-start(bf16[4,128,128]{2,1,0:T(8,128)(2,1)S(1)} %pad_maximum_fusion.2), channel_id=1, source_target_pairs={{0,4},{1,5},{2,6},{3,7},{4,0},{5,1},{6,2},{7,3},{8,12},{9,13},{10,... | collective-permute-start | bytes 393224 | tf_op jit(solution)/shard_map/ppermute | solution.py:41
  113.0 11.8 %collective-permute-start.3 = (bf16[8,128,128]{2,1,0:T(8,128)(2,1)S(1)}, bf16[8,128,128]{2,1,0:T(8,128)(2,1)S(1)}, u32[]{:S(2)}, u32[]{:S(2)}) collective-permute-start(bf16[8,128,128]{2,1,0:T(8,128)(2,1)S(1)} %pad_maximum_fusion), channel_id=1, source_target_pairs={{0,2},{1,3},{2,0},{3,1},{4,6},{5,7},{6,4},{7,5},{8,10},{9,11},{10,... | collective-permute-start | bytes 786440 | tf_op jit(solution)/shard_map/ppermute | solution.py:41
  125.7 13.0 %collective-permute-start.4 = (bf16[16,128,128]{2,1,0:T(8,128)(2,1)}, bf16[16,128,128]{2,1,0:T(8,128)(2,1)S(1)}, u32[]{:S(2)}, u32[]{:S(2)}) collective-permute-start(bf16[16,128,128]{2,1,0:T(8,128)(2,1)} %get-tuple-element.15), channel_id=1, source_target_pairs={{0,1},{1,0},{2,3},{3,2},{4,5},{5,4},{6,7},{7,6},{8,9},{9,8},{10,11... | collective-permute-start | bytes 1572872 | tf_op jit(solution)/shard_map/ppermute | solution.py:41
  153.9 8.7 %collective-permute-start.5 = (bf16[1,128,128]{2,1,0:T(8,128)(2,1)S(1)}, bf16[1,128,128]{2,1,0:T(8,128)(2,1)S(1)}, u32[]{:S(2)}, u32[]{:S(2)}) collective-permute-start(bf16[1,128,128]{2,1,0:T(8,128)(2,1)S(1)} %get-tuple-element.31), channel_id=1, source_target_pairs={{0,256},{32,288},{64,320},{96,352},{128,384},{160,416},{192,448},{... | collective-permute-start | bytes 98312 | tf_op jit(solution)/shard_map/ppermute | solution.py:41
  162.6 15.1 %collective-permute-start.6 = (bf16[2,128,128]{2,1,0:T(8,128)(2,1)S(1)}, bf16[2,128,128]{2,1,0:T(8,128)(2,1)S(1)}, u32[]{:S(2)}, u32[]{:S(2)}) collective-permute-start(bf16[2,128,128]{2,1,0:T(8,128)(2,1)S(1)} %pad_maximum_fusion.5), channel_id=1, source_target_pairs={{0,128},{32,160},{64,192},{96,224},{128,0},{160,32},{192,64},{224,... | collective-permute-start | bytes 196616 | tf_op jit(solution)/shard_map/ppermute | solution.py:41
  166.0 60.6 %all-to-all-start.3 = ((bf16[32,128,128]{1,2,0:T(8,128)(2,1)}), bf16[32,128,128]{1,2,0:T(8,128)(2,1)S(1)}, u32[]{:S(2)}, u32[]{:S(2)}) async-start(bf16[32,128,128]{1,2,0:T(8,128)(2,1)} %broadcast_in_dim.57), calls=%async_computation.3 | async-start | bytes 2097152 | tf_op jit(solution)/shard_map/all_to_all | solution.py:34
  177.7 5.7 %collective-permute-start.7 = (bf16[4,128,128]{2,1,0:T(8,128)(2,1)S(1)}, bf16[4,128,128]{2,1,0:T(8,128)(2,1)S(1)}, u32[]{:S(2)}, u32[]{:S(2)}) collective-permute-start(bf16[4,128,128]{2,1,0:T(8,128)(2,1)S(1)} %pad_maximum_fusion.3), channel_id=1, source_target_pairs={{0,64},{32,96},{64,0},{96,32},{128,192},{160,224},{192,128},{224,1... | collective-permute-start | bytes 393224 | tf_op jit(solution)/shard_map/ppermute | solution.py:41
  183.4 26.1 %collective-permute-start.8 = (bf16[8,128,128]{2,1,0:T(8,128)(2,1)S(1)}, bf16[8,128,128]{2,1,0:T(8,128)(2,1)S(1)}, u32[]{:S(2)}, u32[]{:S(2)}) collective-permute-start(bf16[8,128,128]{2,1,0:T(8,128)(2,1)S(1)} %pad_maximum_fusion.1), channel_id=1, source_target_pairs={{0,512},{32,544},{64,576},{96,608},{128,640},{160,672},{192,704},{... | collective-permute-start | bytes 786440 | tf_op jit(solution)/shard_map/ppermute | solution.py:41
  210.3 4.0 %collective-permute-start.9 = (bf16[16,128,128]{2,1,0:T(8,128)(2,1)}, bf16[16,128,128]{2,1,0:T(8,128)(2,1)S(1)}, u32[]{:S(2)}, u32[]{:S(2)}) collective-permute-start(bf16[16,128,128]{2,1,0:T(8,128)(2,1)} %get-tuple-element.13), channel_id=1, source_target_pairs={{0,32},{32,0},{64,96},{96,64},{128,160},{160,128},{192,224},{224,1... | collective-permute-start | bytes 1572872 | tf_op jit(solution)/shard_map/ppermute | solution.py:41

commit v3 on v2

--- a/solution.py
+++ b/solution.py
@@ -1,6 +1,8 @@
 import jax
 import jax.numpy as jnp
 from jax import lax
+from jax.experimental import pallas as pl
+from jax.experimental.pallas import tpu as pltpu
 from jax.sharding import PartitionSpec as P
 
 NB = 4096
@@ -50,6 +52,61 @@
     return (block // (Z * CORE) * CORE + block % CORE) * Z + block // CORE % Z
 
 
+ROWS_A_STEP = 16
+ROWS_A_DOT = 256
+IN_VMEM = pl.BlockSpec(memory_space=pltpu.VMEM)
+
+
+def place_kernel(index_ref, rows_ref, placed_ref, wide, placed):
+    wide[...] = rows_ref[...].astype(jnp.float32)
+
+    def some(step, carry):
+        for i in range(ROWS_A_STEP):
+            row = step * ROWS_A_STEP + i
+            placed[pl.ds(row, 1), :] = wide[pl.ds(index_ref[row], 1), :]
+        return carry
+
+    lax.fori_loop(0, rows_ref.shape[0] // ROWS_A_STEP, some, 0)
+    placed_ref[...] = placed[...].astype(placed_ref.dtype)
+
+
+def place(rows, index):
+    return pl.pallas_call(
+        place_kernel,
+        out_shape=jax.ShapeDtypeStruct(rows.shape, rows.dtype),
+        in_specs=[pl.BlockSpec(memory_space=pltpu.SMEM), IN_VMEM],
+        out_specs=IN_VMEM,
+        scratch_shapes=[pltpu.VMEM(rows.shape, jnp.float32)] * 2,
+        compiler_params=pltpu.CompilerParams(vmem_limit_bytes=12 << 20),
+        cost_estimate=pl.CostEstimate(flops=0, bytes_accessed=12 * rows.size, transcendentals=0),
+        name="place_rows",
+    )(index, rows)
+
+
+def apply_kernel(theta_ref, coeffs_ref, applied_ref):
+    applied_ref[...] = jnp.dot(
+        theta_ref[...], coeffs_ref[...], preferred_element_type=jnp.float32
+    ).astype(applied_ref.dtype)
+
+
+def apply(theta, coeffs):
+    rows, depth, columns = *theta.shape, coeffs.shape[1]
+    return pl.pallas_call(
+        apply_kernel,
+        out_shape=jax.ShapeDtypeStruct((rows, columns), theta.dtype),
+        grid=(rows // ROWS_A_DOT,),
+        in_specs=[
+            pl.BlockSpec((ROWS_A_DOT, depth), lambda i: (i, 0)),
+            pl.BlockSpec((depth, columns), lambda i: (0, 0), pipeline_mode=pl.Buffered(1)),
+        ],
+        out_specs=pl.BlockSpec((ROWS_A_DOT, columns), lambda i: (i, 0)),
+        cost_estimate=pl.CostEstimate(
+            flops=2 * rows * depth * columns, bytes_accessed=2 * (theta.size + coeffs.size), transcendentals=0
+        ),
+        name="apply_theta",
+    )(theta, coeffs)
+
+
 def take(rows, index):
     return jnp.take(rows, index, axis=0, mode="clip")
 
@@ -80,7 +137,7 @@
     for k in range(band_count):
         blocks[doubled_place(k, BAND_BITS)] = k
     blocks = jnp.asarray(blocks, jnp.int32) ^ lax.axis_index("band")
-    sampled = take(gathered, take(placing.reshape(band_count, own), blocks).reshape(point_count))
+    sampled = place(gathered, take(placing.reshape(band_count, own), blocks).reshape(point_count))
     product = lax.dot_general(
         metric_rows,
         sampled.reshape(grid_count, own, -1),
@@ -92,7 +149,7 @@
     squared = (density * density).astype(jnp.bfloat16)
     squared = exchange_band(spread(squared, band_count))
     order = order.reshape(Y, Z, CORE, own).swapaxes(1, 2).reshape(point_count)
-    products = take(products, doubled_place(order // own ^ me, GRID_BITS) * own + order % own)
+    products = place(products, doubled_place(order // own ^ me, GRID_BITS) * own + order % own)
     coeffs = lax.dot_general(
         squared,
         products.reshape(grid_count, own, -1),
@@ -100,7 +157,7 @@
         preferred_element_type=jnp.float32,
     ).astype(jnp.bfloat16)
     coeffs = gather_yc(gather_z(coeffs)).reshape(point_count, -1)
-    return jnp.dot(theta, coeffs, preferred_element_type=jnp.float32).astype(jnp.bfloat16)
+    return apply(theta, coeffs)
 
 
 def solution(mesh):

time: 268 us -> 246 us (0.918)
  local copies, waits for them, and re-layouts: 37.2 us -> 9.15 us
  Pallas kernels: 0 us -> 17.1 us
  waiting for transfers between devices: 83.4 us -> 68 us
  starting transfers between devices: 60.7 us -> 75.6 us
  matrix products: 10.4 us -> 2.29 us
    gather x5 -> x3, local copies, waits for them, and re-layouts: 26.3 us -> 1.99 us  [take(): return jnp.take(rows, index, axis=0, mode='clip')]
    ppermute x10, waiting for transfers between devices: 83.4 us -> 60.4 us  [gather_doubling(): lax.ppermute(x, axis, [(j, j ^ bit) for j in range(count)])]
    ppermute x10, starting transfers between devices: 32.5 us -> 51.9 us  [gather_doubling(): lax.ppermute(x, axis, [(j, j ^ bit) for j in range(count)])]
    pallas_call x0 -> x3, Pallas kernels: none -> 17.1 us  [the longest x2 10.7 us: place(): pl.pallas_call(place_kernel, out_shape=jax.ShapeDtypeStruct(rows.shape, r...]
    all_to_all x1, waiting for transfers between devices: 0.01 us -> 7.54 us  [gather_yc(): lax.all_to_all(spread(along_z, Y * CORE), 'grid', 0, 0, axis_index_groups...]
    dot_general x1 -> x0, matrix products: 6.3 us -> none  [shards(): jnp.dot(theta, coeffs, preferred_element_type=jnp.float32)]
    all_to_all x2, starting transfers between devices: 22.4 us -> 17.9 us  [exchange_band(): return lax.all_to_all(blocks, 'band', 0, 0, tiled=True)]
  transfers between devices with their start and end apart: 13 -> 13, of which waited for: 8 -> 11; matrix products, arithmetic and copies ran while one was open for 17% -> 6% of each run, Pallas kernels for 0% -> 4%
where the time goes in v3:
time: 246 us; the launch traced here: 245 us
  starting transfers between devices  75.6 us (31%)
  waiting for transfers between devices  68 us (28%)
  blocking collectives  59.3 us (24%)
  Pallas kernels  17.1 us (7%)
  other arithmetic  13.5 us (5%)
  local copies, waits for them, and re-layouts  9.15 us (4%)
    ppermute x10, waiting for transfers between devices, gather_doubling(): lax.ppermute(x, axis, [(j, j ^ bit) for j in range(count)])  60.4 us
    ppermute x10, starting transfers between devices, gather_doubling(): lax.ppermute(x, axis, [(j, j ^ bit) for j in range(count)])  51.9 us
    all_to_all x2, blocking collectives, gather_z(): lax.all_to_all(spread(x, Z), 'grid', 0, 0, axis_index_groups=Z_GROUPS, ti...  42.2 us
    all_to_all x2, starting transfers between devices, exchange_band(): return lax.all_to_all(blocks, 'band', 0, 0, tiled=True)  17.9 us
    all_to_all x1, blocking collectives, gather_yc(): lax.all_to_all(spread(along_z, Y * CORE), 'grid', 0, 0, axis_index_groups...  17.1 us
    pallas_call x2, Pallas kernels, place(): pl.pallas_call(place_kernel, out_shape=jax.ShapeDtypeStruct(rows.shape, r...  10.7 us
    all_to_all x1, waiting for transfers between devices, gather_yc(): lax.all_to_all(spread(along_z, Y * CORE), 'grid', 0, 0, axis_index_groups...  7.54 us
    pallas_call x1, Pallas kernels, apply(): pl.pallas_call(apply_kernel, out_shape=jax.ShapeDtypeStruct((rows, column...  6.38 us
  transfers between devices with their start and end apart: 13, of which 11 were waited for; matrix products, arithmetic and copies ran while one was open for 6% of the time, Pallas kernels for 4%

profile of v3, /device:TPU:1, one launch (start us, length us, event | category | flops | bytes accessed | tf_op | source)
XLA Modules:
  0.0 245.2 jit_solution(9803606300454430974)
XLA Ops:
  0.0 5.9 %sort.30 = (s32[4096]{0:T(1024)S(1)}, s32[4096]{0:T(1024)S(1)}) sort(s32[4096]{0:T(1024)} %param.6, s32[4096]{0:T(1024)S(1)} %iota.5), dimensions={0}, to_apply=%region_0.0 | sort | flops 49152 | bytes 65536 | tf_op jit(solution)/shard_map/sort | solution.py:121
  5.9 0.7 broadcast_xor_fusion
  6.7 0.7 gather_fusion
  7.4 27.5 %all_to_all.30 = bf16[8,128,128]{2,1,0:T(8,128)(2,1)S(1)} all-to-all(bf16[8,128,128]{2,1,0:T(8,128)(2,1)S(1)} %broadcast_in_dim.27), channel_id=1, replica_groups={{0,64,128,192,256,320,384,448},{32,96,160,224,288,352,416,480},{512,576..., dimensions={0} | all-to-all | bytes 524288 | tf_op jit(solution)/shard_map/all_to_all | solution.py:27
  35.0 1.2 broadcast_in_dim.50
  36.2 5.8 %all-to-all-start.1 = ((bf16[4,8,128,128]{3,2,1,0:T(8,128)(2,1)}), bf16[4,8,128,128]{3,2,1,0:T(8,128)(2,1)S(1)}, u32[]{:S(2)}, u32[]{:S(2)}) async-start(bf16[4,8,128,128]{3,2,1,0:T(8,128)(2,1)} %broadcast_in_dim.50), calls=%async_computation.1 | async-start | bytes 2097152 | tf_op jit(solution)/shard_map/all_to_all | solution.py:31
  42.0 5.8 %sort.31 = (s32[4096]{0:T(1024)}, s32[4096]{0:T(1024)S(1)}) sort(s32[4096]{0:T(1024)S(1)} %get-tuple-element.9, s32[4096]{0:T(1024)S(1)} %iota.6), dimensions={0}, to_apply=%region_1.2 | sort | flops 49152 | bytes 65536 | tf_op jit(solution)/shard_map/sort | solution.py:127
  47.9 7.5 %all-to-all-done.1 = bf16[4,8,128,128]{3,2,1,0:T(8,128)(2,1)S(1)} async-done(((bf16[4,8,128,128]{3,2,1,0:T(8,128)(2,1)}), bf16[4,8,128,128]{3,2,1,0:T(8,128)(2,1)S(1)}, u32[]{:S(2)}, u32[]{:S(2)}) %all-to-all-start.1) | async-done | bytes 1048608 | tf_op jit(solution)/shard_map/all_to_all | solution.py:31
  55.5 0.7 gather_fusion.1
  56.2 1.4 convolution_convert_fusion
  57.6 12.6 %all-to-all-start.2 = ((bf16[32,128,128]{2,1,0:T(8,128)(2,1)}), bf16[32,128,128]{2,1,0:T(8,128)(2,1)S(1)}, u32[]{:S(2)}, u32[]{:S(2)}) async-start(bf16[32,128,128]{2,1,0:T(8,128)(2,1)} %bitcast.1), calls=%async_computation.2 | async-start | bytes 2097152 | tf_op jit(solution)/shard_map/all_to_all | solution.py:36
  70.2 0.6 constant_dynamic-update-slice_fusion.4
  70.8 7.0 %collective-permute-start = (bf16[1,128,128]{2,1,0:T(8,128)(2,1)S(1)}, bf16[1,128,128]{2,1,0:T(8,128)(2,1)S(1)}, u32[]{:S(2)}, u32[]{:S(2)}) collective-permute-start(bf16[1,128,128]{2,1,0:T(8,128)(2,1)S(1)} %get-tuple-element.12), channel_id=1, source_target_pairs={{0,16},{1,17},{2,18},{3,19},{4,20},{5,21},{6,22},{7,23},{8,24},{9,... | collective-permute-start | bytes 98312 | tf_op jit(solution)/shard_map/ppermute | solution.py:43
  77.9 12.8 %collective-permute-done = bf16[1,128,128]{2,1,0:T(8,128)(2,1)S(1)} collective-permute-done((bf16[1,128,128]{2,1,0:T(8,128)(2,1)S(1)}, bf16[1,128,128]{2,1,0:T(8,128)(2,1)S(1)}, u32[]{:S(2)}, u32[]{:S(2)}) %collective-permute-start) | collective-permute-done | bytes 32800 | tf_op jit(solution)/shard_map/ppermute | solution.py:43
  90.7 13.2 %collective-permute-start.1 = (bf16[2,128,128]{2,1,0:T(8,128)(2,1)S(1)}, bf16[2,128,128]{2,1,0:T(8,128)(2,1)S(1)}, u32[]{:S(2)}, u32[]{:S(2)}) collective-permute-start(bf16[2,128,128]{2,1,0:T(8,128)(2,1)S(1)} %pad_maximum_fusion.4), channel_id=1, source_target_pairs={{0,8},{1,9},{2,10},{3,11},{4,12},{5,13},{6,14},{7,15},{8,0},{9,1},... | collective-permute-start | bytes 196616 | tf_op jit(solution)/shard_map/ppermute | solution.py:43
  103.9 1.6 collective-permute-done.1
  105.6 7.3 %collective-permute-start.2 = (bf16[4,128,128]{2,1,0:T(8,128)(2,1)S(1)}, bf16[4,128,128]{2,1,0:T(8,128)(2,1)S(1)}, u32[]{:S(2)}, u32[]{:S(2)}) collective-permute-start(bf16[4,128,128]{2,1,0:T(8,128)(2,1)S(1)} %pad_maximum_fusion.2), channel_id=1, source_target_pairs={{0,4},{1,5},{2,6},{3,7},{4,0},{5,1},{6,2},{7,3},{8,12},{9,13},{10,... | collective-permute-start | bytes 393224 | tf_op jit(solution)/shard_map/ppermute | solution.py:43
  112.9 4.3 %collective-permute-done.2 = bf16[4,128,128]{2,1,0:T(8,128)(2,1)S(1)} collective-permute-done((bf16[4,128,128]{2,1,0:T(8,128)(2,1)S(1)}, bf16[4,128,128]{2,1,0:T(8,128)(2,1)S(1)}, u32[]{:S(2)}, u32[]{:S(2)}) %collective-permute-start.2) | collective-permute-done | bytes 131104 | tf_op jit(solution)/shard_map/ppermute | solution.py:43
  117.2 5.4 %collective-permute-start.3 = (bf16[8,128,128]{2,1,0:T(8,128)(2,1)S(1)}, bf16[8,128,128]{2,1,0:T(8,128)(2,1)S(1)}, u32[]{:S(2)}, u32[]{:S(2)}) collective-permute-start(bf16[8,128,128]{2,1,0:T(8,128)(2,1)S(1)} %pad_maximum_fusion), channel_id=1, source_target_pairs={{0,2},{1,3},{2,0},{3,1},{4,6},{5,7},{6,4},{7,5},{8,10},{9,11},{10,... | collective-permute-start | bytes 786440 | tf_op jit(solution)/shard_map/ppermute | solution.py:43
  122.6 0.6 constant_dynamic-update-slice_fusion.3
  123.2 0.7 constant_dynamic-update-slice_fusion.2
  123.9 0.7 constant_dynamic-update-slice_fusion.1
  124.6 10.3 %collective-permute-done.3 = bf16[8,128,128]{2,1,0:T(8,128)(2,1)S(1)} collective-permute-done((bf16[8,128,128]{2,1,0:T(8,128)(2,1)S(1)}, bf16[8,128,128]{2,1,0:T(8,128)(2,1)S(1)}, u32[]{:S(2)}, u32[]{:S(2)}) %collective-permute-start.3) | collective-permute-done | bytes 262176 | tf_op jit(solution)/shard_map/ppermute | solution.py:43
  134.8 0.8 constant_dynamic-update-slice_fusion
  135.6 1.9 collective-permute-start.4
  137.6 0.6 gather_fusion.2
  138.5 1.2 broadcast_in_dim.52
  139.7 5.3 %all-to-all-start.3 = ((bf16[32,128,128]{1,2,0:T(8,128)(2,1)}), bf16[32,128,128]{1,2,0:T(8,128)(2,1)S(1)}, u32[]{:S(2)}, u32[]{:S(2)}) async-start(bf16[32,128,128]{1,2,0:T(8,128)(2,1)} %broadcast_in_dim.52), calls=%async_computation.3 | async-start | bytes 2097152 | tf_op jit(solution)/shard_map/all_to_all | solution.py:36
  145.0 9.1 %collective-permute-done.4 = bf16[16,128,128]{2,1,0:T(8,128)(2,1)} collective-permute-done((bf16[16,128,128]{2,1,0:T(8,128)(2,1)}, bf16[16,128,128]{2,1,0:T(8,128)(2,1)}, u32[]{:S(2)}, u32[]{:S(2)}) %collective-permute-start.4) | collective-permute-done | bytes 524320 | tf_op jit(solution)/shard_map/ppermute | solution.py:43
  154.1 1.1 constant_dynamic-update-slice_fusion.5
  155.3 5.4 %place_rows.2 = bf16[4096,128]{1,0:T(8,128)(2,1)S(1)} custom-call(s32[4096]{0:T(1024)S(1)} %bitcast.40, bf16[4096,128]{1,0:T(8,128)(2,1)S(1)} %bitcast.36), custom_call_target="tpu_custom_call" | custom-call | bytes 6291456 | tf_op jit(solution)/shard_map/place_rows/pallas_call | solution.py:74
  160.6 0.5 constant_dynamic-update-slice_fusion.15
  161.1 1.9 collective-permute-start.5
  163.0 7.0 %collective-permute-done.5 = bf16[1,128,128]{2,1,0:T(8,128)(2,1)S(1)} collective-permute-done((bf16[1,128,128]{2,1,0:T(8,128)(2,1)S(1)}, bf16[1,128,128]{2,1,0:T(8,128)(2,1)S(1)}, u32[]{:S(2)}, u32[]{:S(2)}) %collective-permute-start.5) | collective-permute-done | bytes 32800 | tf_op jit(solution)/shard_map/ppermute | solution.py:43
  170.0 1.9 collective-permute-start.6
  171.9 4.9 %collective-permute-done.6 = bf16[2,128,128]{2,1,0:T(8,128)(2,1)S(1)} collective-permute-done((bf16[2,128,128]{2,1,0:T(8,128)(2,1)S(1)}, bf16[2,128,128]{2,1,0:T(8,128)(2,1)S(1)}, u32[]{:S(2)}, u32[]{:S(2)}) %collective-permute-start.6) | collective-permute-done | bytes 65568 | tf_op jit(solution)/shard_map/ppermute | solution.py:43
  176.8 1.9 collective-permute-start.7
  178.8 4.0 %collective-permute-done.7 = bf16[4,128,128]{2,1,0:T(8,128)(2,1)S(1)} collective-permute-done((bf16[4,128,128]{2,1,0:T(8,128)(2,1)S(1)}, bf16[4,128,128]{2,1,0:T(8,128)(2,1)S(1)}, u32[]{:S(2)}, u32[]{:S(2)}) %collective-permute-start.7) | collective-permute-done | bytes 131104 | tf_op jit(solution)/shard_map/ppermute | solution.py:43
  182.8 1.9 collective-permute-start.8
  184.8 5.1 %collective-permute-done.8 = bf16[8,128,128]{2,1,0:T(8,128)(2,1)S(1)} collective-permute-done((bf16[8,128,128]{2,1,0:T(8,128)(2,1)S(1)}, bf16[8,128,128]{2,1,0:T(8,128)(2,1)S(1)}, u32[]{:S(2)}, u32[]{:S(2)}) %collective-permute-start.8) | collective-permute-done | bytes 262176 | tf_op jit(solution)/shard_map/ppermute | solution.py:43
  190.0 9.4 %collective-permute-start.9 = (bf16[16,128,128]{2,1,0:T(8,128)(2,1)S(1)}, bf16[16,128,128]{2,1,0:T(8,128)(2,1)S(1)}, u32[]{:S(2)}, u32[]{:S(2)}) collective-permute-start(bf16[16,128,128]{2,1,0:T(8,128)(2,1)S(1)} %get-tuple-element.13), channel_id=1, source_target_pairs={{0,32},{32,0},{64,96},{96,64},{128,160},{160,128},{192,224},{224,1... | collective-permute-start | bytes 1572872 | tf_op jit(solution)/shard_map/ppermute | solution.py:43
  199.5 1.4 collective-permute-done.9
  201.0 5.4 %place_rows.3 = bf16[4096,128]{1,0:T(8,128)(2,1)S(1)} custom-call(s32[4096]{0:T(1024)S(1)} %fusion.20.index_ref, bf16[4096,128]{1,0:T(8,128)(2,1)S(1)} %bitcast.39), custom_call_target="tpu_custom_call" | custom-call | bytes 6291456 | tf_op jit(solution)/shard_map/place_rows/pallas_call | solution.py:74
  206.4 0.4 fusion.1
  206.9 14.7 %all_to_all.31 = bf16[8,128,128]{2,1,0:T(8,128)(2,1)S(1)} all-to-all(bf16[8,128,128]{2,1,0:T(8,128)(2,1)S(1)} %broadcast_in_dim.56), channel_id=1, replica_groups={{0,64,128,192,256,320,384,448},{32,96,160,224,288,352,416,480},{512,576..., dimensions={0} | all-to-all | bytes 524288 | tf_op jit(solution)/shard_map/all_to_all | solution.py:27
  221.6 0.2 broadcast_in_dim.57
  221.8 17.1 %all_to_all.32 = bf16[4,8,128,128]{3,2,1,0:T(8,128)(2,1)} all-to-all(bf16[4,8,128,128]{3,2,1,0:T(8,128)(2,1)S(1)} %broadcast_in_dim.57), channel_id=1, replica_groups={{0,32,512,544},{64,96,576,608},{128,160,640,672},{192,224,704,736},{256..., dimensions={0} | all-to-all | bytes 2097152 | tf_op jit(solution)/shard_map/all_to_all | solution.py:31
  238.9 6.4 %apply_theta.1 = bf16[1024,128]{1,0:T(8,128)(2,1)} custom-call(bf16[1024,4096]{1,0:T(8,128)(2,1)} %theta_ref.1, bf16[4096,128]{1,0:T(8,128)(2,1)} %bitcast.41), custom_call_target="tpu_custom_call" | custom-call | flops 1073741824 | bytes 9437184 | tf_op jit(solution)/shard_map/apply_theta/pallas_call | solution.py:94
  (33 shorter events, 1.1 us)
Async XLA Ops:
  0.0 6.7 %copy-start = (bf16[1024,128]{1,0:T(8,128)(2,1)S(1)}, bf16[1024,128]{1,0:T(8,128)(2,1)}, u32[]{:S(2)}) copy-start(bf16[1024,128]{1,0:T(8,128)(2,1)} %param.5) | copy-start | bytes 786436
  36.2 19.3 %all-to-all-start.1 = ((bf16[4,8,128,128]{3,2,1,0:T(8,128)(2,1)}), bf16[4,8,128,128]{3,2,1,0:T(8,128)(2,1)S(1)}, u32[]{:S(2)}, u32[]{:S(2)}) async-start(bf16[4,8,128,128]{3,2,1,0:T(8,128)(2,1)} %broadcast_in_dim.50), calls=%async_computation.1 | async-start | bytes 2097152 | tf_op jit(solution)/shard_map/all_to_all | solution.py:31
  56.2 14.0 %copy-start.1 = (f32[128,128]{1,0:T(8,128)S(1)}, f32[128,128]{1,0:T(8,128)}, u32[]{:S(2)}) copy-start(f32[128,128]{1,0:T(8,128)} %param.8) | copy-start | bytes 196612
  57.6 80.6 %all-to-all-start.2 = ((bf16[32,128,128]{2,1,0:T(8,128)(2,1)}), bf16[32,128,128]{2,1,0:T(8,128)(2,1)S(1)}, u32[]{:S(2)}, u32[]{:S(2)}) async-start(bf16[32,128,128]{2,1,0:T(8,128)(2,1)} %bitcast.1), calls=%async_computation.2 | async-start | bytes 2097152 | tf_op jit(solution)/shard_map/all_to_all | solution.py:36
  70.8 19.9 %collective-permute-start = (bf16[1,128,128]{2,1,0:T(8,128)(2,1)S(1)}, bf16[1,128,128]{2,1,0:T(8,128)(2,1)S(1)}, u32[]{:S(2)}, u32[]{:S(2)}) collective-permute-start(bf16[1,128,128]{2,1,0:T(8,128)(2,1)S(1)} %get-tuple-element.12), channel_id=1, source_target_pairs={{0,16},{1,17},{2,18},{3,19},{4,20},{5,21},{6,22},{7,23},{8,24},{9,... | collective-permute-start | bytes 98312 | tf_op jit(solution)/shard_map/ppermute | solution.py:43
  90.7 14.9 %collective-permute-start.1 = (bf16[2,128,128]{2,1,0:T(8,128)(2,1)S(1)}, bf16[2,128,128]{2,1,0:T(8,128)(2,1)S(1)}, u32[]{:S(2)}, u32[]{:S(2)}) collective-permute-start(bf16[2,128,128]{2,1,0:T(8,128)(2,1)S(1)} %pad_maximum_fusion.4), channel_id=1, source_target_pairs={{0,8},{1,9},{2,10},{3,11},{4,12},{5,13},{6,14},{7,15},{8,0},{9,1},... | collective-permute-start | bytes 196616 | tf_op jit(solution)/shard_map/ppermute | solution.py:43
  105.6 11.6 %collective-permute-start.2 = (bf16[4,128,128]{2,1,0:T(8,128)(2,1)S(1)}, bf16[4,128,128]{2,1,0:T(8,128)(2,1)S(1)}, u32[]{:S(2)}, u32[]{:S(2)}) collective-permute-start(bf16[4,128,128]{2,1,0:T(8,128)(2,1)S(1)} %pad_maximum_fusion.2), channel_id=1, source_target_pairs={{0,4},{1,5},{2,6},{3,7},{4,0},{5,1},{6,2},{7,3},{8,12},{9,13},{10,... | collective-permute-start | bytes 393224 | tf_op jit(solution)/shard_map/ppermute | solution.py:43
  117.2 17.6 %collective-permute-start.3 = (bf16[8,128,128]{2,1,0:T(8,128)(2,1)S(1)}, bf16[8,128,128]{2,1,0:T(8,128)(2,1)S(1)}, u32[]{:S(2)}, u32[]{:S(2)}) collective-permute-start(bf16[8,128,128]{2,1,0:T(8,128)(2,1)S(1)} %pad_maximum_fusion), channel_id=1, source_target_pairs={{0,2},{1,3},{2,0},{3,1},{4,6},{5,7},{6,4},{7,5},{8,10},{9,11},{10,... | collective-permute-start | bytes 786440 | tf_op jit(solution)/shard_map/ppermute | solution.py:43
  135.6 18.5 %collective-permute-start.4 = (bf16[16,128,128]{2,1,0:T(8,128)(2,1)}, bf16[16,128,128]{2,1,0:T(8,128)(2,1)}, u32[]{:S(2)}, u32[]{:S(2)}) collective-permute-start(bf16[16,128,128]{2,1,0:T(8,128)(2,1)} %get-tuple-element.15), channel_id=1, source_target_pairs={{0,1},{1,0},{2,3},{3,2},{4,5},{5,4},{6,7},{7,6},{8,9},{9,8},{10,11... | collective-permute-start | bytes 1572872 | tf_op jit(solution)/shard_map/ppermute | solution.py:43
  139.7 66.7 %all-to-all-start.3 = ((bf16[32,128,128]{1,2,0:T(8,128)(2,1)}), bf16[32,128,128]{1,2,0:T(8,128)(2,1)S(1)}, u32[]{:S(2)}, u32[]{:S(2)}) async-start(bf16[32,128,128]{1,2,0:T(8,128)(2,1)} %broadcast_in_dim.52), calls=%async_computation.3 | async-start | bytes 2097152 | tf_op jit(solution)/shard_map/all_to_all | solution.py:36
  161.1 8.9 %collective-permute-start.5 = (bf16[1,128,128]{2,1,0:T(8,128)(2,1)S(1)}, bf16[1,128,128]{2,1,0:T(8,128)(2,1)S(1)}, u32[]{:S(2)}, u32[]{:S(2)}) collective-permute-start(bf16[1,128,128]{2,1,0:T(8,128)(2,1)S(1)} %get-tuple-element.31), channel_id=1, source_target_pairs={{0,256},{32,288},{64,320},{96,352},{128,384},{160,416},{192,448},{... | collective-permute-start | bytes 98312 | tf_op jit(solution)/shard_map/ppermute | solution.py:43
  170.0 6.8 %collective-permute-start.6 = (bf16[2,128,128]{2,1,0:T(8,128)(2,1)S(1)}, bf16[2,128,128]{2,1,0:T(8,128)(2,1)S(1)}, u32[]{:S(2)}, u32[]{:S(2)}) collective-permute-start(bf16[2,128,128]{2,1,0:T(8,128)(2,1)S(1)} %pad_maximum_fusion.5), channel_id=1, source_target_pairs={{0,128},{32,160},{64,192},{96,224},{128,0},{160,32},{192,64},{224,... | collective-permute-start | bytes 196616 | tf_op jit(solution)/shard_map/ppermute | solution.py:43
  176.8 5.9 %collective-permute-start.7 = (bf16[4,128,128]{2,1,0:T(8,128)(2,1)S(1)}, bf16[4,128,128]{2,1,0:T(8,128)(2,1)S(1)}, u32[]{:S(2)}, u32[]{:S(2)}) collective-permute-start(bf16[4,128,128]{2,1,0:T(8,128)(2,1)S(1)} %pad_maximum_fusion.3), channel_id=1, source_target_pairs={{0,64},{32,96},{64,0},{96,32},{128,192},{160,224},{192,128},{224,1... | collective-permute-start | bytes 393224 | tf_op jit(solution)/shard_map/ppermute | solution.py:43
  182.8 7.1 %collective-permute-start.8 = (bf16[8,128,128]{2,1,0:T(8,128)(2,1)S(1)}, bf16[8,128,128]{2,1,0:T(8,128)(2,1)S(1)}, u32[]{:S(2)}, u32[]{:S(2)}) collective-permute-start(bf16[8,128,128]{2,1,0:T(8,128)(2,1)S(1)} %pad_maximum_fusion.1), channel_id=1, source_target_pairs={{0,512},{32,544},{64,576},{96,608},{128,640},{160,672},{192,704},{... | collective-permute-start | bytes 786440 | tf_op jit(solution)/shard_map/ppermute | solution.py:43
  190.0 10.9 %collective-permute-start.9 = (bf16[16,128,128]{2,1,0:T(8,128)(2,1)S(1)}, bf16[16,128,128]{2,1,0:T(8,128)(2,1)S(1)}, u32[]{:S(2)}, u32[]{:S(2)}) collective-permute-start(bf16[16,128,128]{2,1,0:T(8,128)(2,1)S(1)} %get-tuple-element.13), channel_id=1, source_target_pairs={{0,32},{32,0},{64,96},{96,64},{128,160},{160,128},{192,224},{224,1... | collective-permute-start | bytes 1572872 | tf_op jit(solution)/shard_map/ppermute | solution.py:43

commit v4 on v3

--- a/solution.py
+++ b/solution.py
@@ -15,8 +15,8 @@
 
 Z_GROUPS = [[grid_index(y, z, c) for z in range(Z)] for y in range(Y) for c in range(CORE)]
 YC_GROUPS = [[grid_index(y, z, c) for y in range(Y) for c in range(CORE)] for z in range(Z)]
-GRID_BITS = (8, 4, 2, 16, 1)
-BAND_BITS = (16, 8, 4, 2, 1)
+GRID_BITS = (16, 8, 4, 2, 1)
+X_BITS, X_FAR, Y_HI = (0, 1, 2, 3), (0, 4), (0, 8, 16, 24)
 
 
 def spread(x, count):
@@ -42,6 +42,16 @@
     for bit in bits:
         x = jnp.concatenate([x, lax.ppermute(x, axis, [(j, j ^ bit) for j in range(count)])])
     return x
+
+
+def swap(x, axis, bit):
+    return lax.ppermute(x, axis, [(i, i ^ bit) for i in range(lax.axis_size(axis))])
+
+
+def gather_metric(block):
+    near = jnp.stack([block, *(swap(block, "band", y) for y in Y_HI[1:])])
+    half = jnp.concatenate([near, swap(near, "band", X_FAR[1])])
+    return [half, *(swap(half, "band", x) for x in X_BITS[1:])]
 
 
 def doubled_place(k, bits):
@@ -83,6 +93,32 @@
     )(index, rows)
 
 
+def multiply_kernel(*refs):
+    *part_refs, rows_ref, product_ref = refs
+    blocks, own, _ = part_refs[0].shape
+    total = jnp.zeros(product_ref.shape, jnp.float32)
+    for i, part_ref in enumerate(part_refs):
+        for block in range(blocks):
+            rows = rows_ref[pl.ds((i * blocks + block) * own, own), :]
+            total += jnp.dot(part_ref[block], rows, preferred_element_type=jnp.float32)
+    product_ref[...] = total.astype(product_ref.dtype)
+
+
+def multiply(parts, rows):
+    own, columns = parts[0].shape[1], rows.shape[1]
+    return pl.pallas_call(
+        multiply_kernel,
+        out_shape=jax.ShapeDtypeStruct((own, columns), rows.dtype),
+        in_specs=[IN_VMEM] * (len(parts) + 1),
+        out_specs=IN_VMEM,
+        compiler_params=pltpu.CompilerParams(vmem_limit_bytes=8 << 20),
+        cost_estimate=pl.CostEstimate(
+            flops=2 * own * rows.size, bytes_accessed=4 * rows.size, transcendentals=0
+        ),
+        name="multiply_metric",
+    )(*parts, rows)
+
+
 def apply_kernel(theta_ref, coeffs_ref, applied_ref):
     applied_ref[...] = jnp.dot(
         theta_ref[...], coeffs_ref[...], preferred_element_type=jnp.float32
@@ -122,7 +158,7 @@
     my_rows = lax.dynamic_slice_in_dim(by_owner, me * own, own, 0) - me * row_count
     packed = take(orbitals, my_rows)
     along_z = gather_z(packed)
-    metric_rows = gather_doubling(metric.astype(jnp.bfloat16), "band", BAND_BITS)
+    metric_parts = gather_metric(metric.astype(jnp.bfloat16))
     gathered = gather_yc(along_z).reshape(point_count, -1)
     placing = lax.sort_key_val(order, slots)[1]
     placing = in_gather_order(placing // own) * own + placing % own
@@ -133,17 +169,10 @@
         gathered, my_points, (((1,), (1,)), ((), ())), preferred_element_type=jnp.float32
     ).astype(jnp.bfloat16)
     partial_rows = exchange_band(partial_rows.reshape(grid_count, own, own))
-    blocks = [0] * band_count
-    for k in range(band_count):
-        blocks[doubled_place(k, BAND_BITS)] = k
+    blocks = [x + far + y for x in X_BITS for far in X_FAR for y in Y_HI]
     blocks = jnp.asarray(blocks, jnp.int32) ^ lax.axis_index("band")
     sampled = place(gathered, take(placing.reshape(band_count, own), blocks).reshape(point_count))
-    product = lax.dot_general(
-        metric_rows,
-        sampled.reshape(grid_count, own, -1),
-        (((0, 2), (0, 1)), ((), ())),
-        preferred_element_type=jnp.float32,
-    ).astype(jnp.bfloat16)
+    product = multiply(metric_parts, sampled)
     products = gather_doubling(product, "grid", GRID_BITS).reshape(point_count, -1)
     density = jnp.sum(partial_rows.astype(jnp.float32), axis=0) * (1.0 / NB)
     squared = (density * density).astype(jnp.bfloat16)

time: 246 us -> 244 us (level)
  the two profiles are of different devices: /device:TPU:1 before, /device:TPU:4 now
where the time goes in v4:
time: 244 us; the launch traced here: 243 us
  waiting for transfers between devices  81.3 us (33%)
  starting transfers between devices  61.9 us (25%)
  blocking collectives  61.4 us (25%)
  Pallas kernels  17.5 us (7%)
  other arithmetic  12.9 us (5%)
  local copies, waits for them, and re-layouts  5.28 us (2%)
    ppermute x7, waiting for transfers between devices, swap(): lax.ppermute(x, axis, [(i, i ^ bit) for i in range(lax.axis_size(axis))])  45.8 us
    all_to_all x2, blocking collectives, gather_z(): lax.all_to_all(spread(x, Z), 'grid', 0, 0, axis_index_groups=Z_GROUPS, ti...  43.2 us
    ppermute x5, waiting for transfers between devices, gather_doubling(): lax.ppermute(x, axis, [(j, j ^ bit) for j in range(count)])  27.1 us
    ppermute x7, starting transfers between devices, swap(): lax.ppermute(x, axis, [(i, i ^ bit) for i in range(lax.axis_size(axis))])  26.3 us
    all_to_all x2, starting transfers between devices, exchange_band(): return lax.all_to_all(blocks, 'band', 0, 0, tiled=True)  21.7 us
    all_to_all x1, blocking collectives, gather_yc(): lax.all_to_all(spread(along_z, Y * CORE), 'grid', 0, 0, axis_index_groups...  18.2 us
    pallas_call x2, Pallas kernels, place(): pl.pallas_call(place_kernel, out_shape=jax.ShapeDtypeStruct(rows.shape, r...  10.7 us
    ppermute x5, starting transfers between devices, gather_doubling(): lax.ppermute(x, axis, [(j, j ^ bit) for j in range(count)])  10.4 us
  transfers between devices with their start and end apart: 15, of which 11 were waited for; matrix products, arithmetic and copies ran while one was open for 4% of the time, Pallas kernels for 5%

profile of v4, /device:TPU:4, one launch (start us, length us, event | category | flops | bytes accessed | tf_op | source)
XLA Modules:
  0.0 242.6 jit_solution(5944959058366219676)
XLA Ops:
  0.0 0.7 broadcast_xor_fusion
  0.7 5.9 %sort.30 = (s32[4096]{0:T(1024)S(1)}, s32[4096]{0:T(1024)S(1)}) sort(s32[4096]{0:T(1024)} %param.6, s32[4096]{0:T(1024)S(1)} %iota.5), dimensions={0}, to_apply=%region_0.0 | sort | flops 49152 | bytes 65536 | tf_op jit(solution)/shard_map/sort | solution.py:157
  6.7 0.7 gather_fusion
  7.4 28.4 %all_to_all.30 = bf16[8,128,128]{2,1,0:T(8,128)(2,1)S(1)} all-to-all(bf16[8,128,128]{2,1,0:T(8,128)(2,1)S(1)} %broadcast_in_dim.25), channel_id=1, replica_groups={{0,64,128,192,256,320,384,448},{32,96,160,224,288,352,416,480},{512,576..., dimensions={0} | all-to-all | bytes 524288 | tf_op jit(solution)/shard_map/all_to_all | solution.py:27
  35.8 1.2 broadcast_in_dim.26
  37.0 3.5 %all-to-all-start.1 = ((bf16[4,8,128,128]{3,2,1,0:T(8,128)(2,1)}), bf16[4,8,128,128]{3,2,1,0:T(8,128)(2,1)S(1)}, u32[]{:S(2)}, u32[]{:S(2)}) async-start(bf16[4,8,128,128]{3,2,1,0:T(8,128)(2,1)} %broadcast_in_dim.26), calls=%async_computation.1 | async-start | bytes 2097152 | tf_op jit(solution)/shard_map/all_to_all | solution.py:31
  40.6 5.8 %sort.31 = (s32[4096]{0:T(1024)}, s32[4096]{0:T(1024)S(1)}) sort(s32[4096]{0:T(1024)S(1)} %get-tuple-element.9, s32[4096]{0:T(1024)S(1)} %iota.6), dimensions={0}, to_apply=%region_1.2 | sort | flops 49152 | bytes 65536 | tf_op jit(solution)/shard_map/sort | solution.py:163
  46.5 8.4 %all-to-all-done.1 = bf16[4,8,128,128]{3,2,1,0:T(8,128)(2,1)S(1)} async-done(((bf16[4,8,128,128]{3,2,1,0:T(8,128)(2,1)}), bf16[4,8,128,128]{3,2,1,0:T(8,128)(2,1)S(1)}, u32[]{:S(2)}, u32[]{:S(2)}) %all-to-all-start.1) | async-done | bytes 1048608 | tf_op jit(solution)/shard_map/all_to_all | solution.py:31
  54.9 0.7 gather_fusion.1
  55.6 1.4 convolution_convert_fusion
  57.0 13.1 %all-to-all-start.2 = ((bf16[32,128,128]{2,1,0:T(8,128)(2,1)}), bf16[32,128,128]{2,1,0:T(8,128)(2,1)S(1)}, u32[]{:S(2)}, u32[]{:S(2)}) async-start(bf16[32,128,128]{2,1,0:T(8,128)(2,1)} %bitcast.1), calls=%async_computation.2 | async-start | bytes 2097152 | tf_op jit(solution)/shard_map/all_to_all | solution.py:36
  70.2 4.3 %collective-permute-start = (bf16[128,128]{1,0:T(8,128)(2,1)S(1)}, bf16[128,128]{1,0:T(8,128)(2,1)S(1)}, u32[]{:S(2)}, u32[]{:S(2)}) collective-permute-start(bf16[128,128]{1,0:T(8,128)(2,1)S(1)} %get-tuple-element.12), channel_id=1, source_target_pairs={{0,8},{1,9},{2,10},{3,11},{4,12},{5,13},{6,14},{7,15},{8,0},{9,1},... | collective-permute-start | bytes 98312 | tf_op jit(solution)/shard_map/ppermute | solution.py:48
  74.5 5.5 %collective-permute-start.1 = (bf16[128,128]{1,0:T(8,128)(2,1)S(1)}, bf16[128,128]{1,0:T(8,128)(2,1)S(1)}, u32[]{:S(2)}, u32[]{:S(2)}) collective-permute-start(bf16[128,128]{1,0:T(8,128)(2,1)S(1)} %get-tuple-element.12), channel_id=1, source_target_pairs={{0,16},{1,17},{2,18},{3,19},{4,20},{5,21},{6,22},{7,23},{8,24},{9,... | collective-permute-start | bytes 98312 | tf_op jit(solution)/shard_map/ppermute | solution.py:48
  80.0 2.4 collective-permute-start.2
  82.5 13.3 %collective-permute-done = bf16[128,128]{1,0:T(8,128)(2,1)S(1)} collective-permute-done((bf16[128,128]{1,0:T(8,128)(2,1)S(1)}, bf16[128,128]{1,0:T(8,128)(2,1)S(1)}, u32[]{:S(2)}, u32[]{:S(2)}) %collective-permute-start) | collective-permute-done | bytes 32800 | tf_op jit(solution)/shard_map/ppermute | solution.py:48
  95.8 5.3 %collective-permute-done.1 = bf16[128,128]{1,0:T(8,128)(2,1)S(1)} collective-permute-done((bf16[128,128]{1,0:T(8,128)(2,1)S(1)}, bf16[128,128]{1,0:T(8,128)(2,1)S(1)}, u32[]{:S(2)}, u32[]{:S(2)}) %collective-permute-start.1) | collective-permute-done | bytes 32800 | tf_op jit(solution)/shard_map/ppermute | solution.py:48
  101.1 4.9 %collective-permute-start.3 = (bf16[4,128,128]{2,1,0:T(8,128)(2,1)S(1)}, bf16[4,128,128]{2,1,0:T(8,128)(2,1)S(1)}, u32[]{:S(2)}, u32[]{:S(2)}) collective-permute-start(bf16[4,128,128]{2,1,0:T(8,128)(2,1)S(1)} %pad_maximum_fusion.1), channel_id=1, source_target_pairs={{0,4},{1,5},{2,6},{3,7},{4,0},{5,1},{6,2},{7,3},{8,12},{9,13},{10,... | collective-permute-start | bytes 393224 | tf_op jit(solution)/shard_map/ppermute | solution.py:48
  106.1 8.8 %collective-permute-done.3 = bf16[4,128,128]{2,1,0:T(8,128)(2,1)S(1)} collective-permute-done((bf16[4,128,128]{2,1,0:T(8,128)(2,1)S(1)}, bf16[4,128,128]{2,1,0:T(8,128)(2,1)S(1)}, u32[]{:S(2)}, u32[]{:S(2)}) %collective-permute-start.3) | collective-permute-done | bytes 131104 | tf_op jit(solution)/shard_map/ppermute | solution.py:48
  114.9 1.9 collective-permute-start.4
  116.9 2.4 collective-permute-start.5
  119.3 4.9 %collective-permute-start.6 = (bf16[8,128,128]{2,1,0:T(8,128)(2,1)S(1)}, bf16[8,128,128]{2,1,0:T(8,128)(2,1)S(1)}, u32[]{:S(2)}, u32[]{:S(2)}) collective-permute-start(bf16[8,128,128]{2,1,0:T(8,128)(2,1)S(1)} %constant_dynamic-update-slice_fusion.refs_0_), channel_id=1, source_target_pairs={{0,3},{1,2},{2,1},{3,0},{4,7},{5,6},{6,5},{7,4},{8,11},{9,10},{10,... | collective-permute-start | bytes 786440 | tf_op jit(solution)/shard_map/ppermute | solution.py:48
  124.2 0.2 convert_reduce_fusion
  124.4 0.1 copy.7
  124.5 1.2 broadcast_in_dim.49
  125.7 8.5 %all-to-all-start.3 = ((bf16[32,128,128]{1,2,0:T(8,128)(2,1)}), bf16[32,128,128]{1,2,0:T(8,128)(2,1)S(1)}, u32[]{:S(2)}, u32[]{:S(2)}) async-start(bf16[32,128,128]{1,2,0:T(8,128)(2,1)} %broadcast_in_dim.49), calls=%async_computation.3 | async-start | bytes 2097152 | tf_op jit(solution)/shard_map/all_to_all | solution.py:36
  134.3 0.6 gather_fusion.2
  134.9 5.4 %place_rows.2.refs_4_ = bf16[4096,128]{1,0:T(8,128)(2,1)S(1)} custom-call(s32[4096]{0:T(1024)S(1)} %bitcast.40, bf16[4096,128]{1,0:T(8,128)(2,1)S(1)} %bitcast.33), custom_call_target="tpu_custom_call" | custom-call | bytes 6291456 | tf_op jit(solution)/shard_map/place_rows/pallas_call | solution.py:84
  140.2 0.1 collective-permute-done.5.refs_2_
  140.4 18.2 %collective-permute-done.6.refs_3_ = bf16[8,128,128]{2,1,0:T(8,128)(2,1)S(1)} collective-permute-done((bf16[8,128,128]{2,1,0:T(8,128)(2,1)S(1)}, bf16[8,128,128]{2,1,0:T(8,128)(2,1)S(1)}, u32[]{:S(2)}, u32[]{:S(2)}) %collective-permute-start.6) | collective-permute-done | bytes 262176 | tf_op jit(solution)/shard_map/ppermute | solution.py:48
  158.5 0.5 multiply_metric.1
  159.0 1.9 collective-permute-start.7
  160.9 4.1 %collective-permute-done.7 = bf16[1,128,128]{2,1,0:T(8,128)(2,1)S(1)} collective-permute-done((bf16[1,128,128]{2,1,0:T(8,128)(2,1)S(1)}, bf16[1,128,128]{2,1,0:T(8,128)(2,1)S(1)}, u32[]{:S(2)}, u32[]{:S(2)}) %collective-permute-start.7) | collective-permute-done | bytes 32800 | tf_op jit(solution)/shard_map/ppermute | solution.py:43
  165.1 2.7 %collective-permute-start.8 = (bf16[2,128,128]{2,1,0:T(8,128)(2,1)S(1)}, bf16[2,128,128]{2,1,0:T(8,128)(2,1)S(1)}, u32[]{:S(2)}, u32[]{:S(2)}) collective-permute-start(bf16[2,128,128]{2,1,0:T(8,128)(2,1)S(1)} %pad_maximum_fusion.3), channel_id=1, source_target_pairs={{0,256},{32,288},{64,320},{96,352},{128,384},{160,416},{192,448},{... | collective-permute-start | bytes 196616 | tf_op jit(solution)/shard_map/ppermute | solution.py:43
  167.8 8.0 %collective-permute-done.8 = bf16[2,128,128]{2,1,0:T(8,128)(2,1)S(1)} collective-permute-done((bf16[2,128,128]{2,1,0:T(8,128)(2,1)S(1)}, bf16[2,128,128]{2,1,0:T(8,128)(2,1)S(1)}, u32[]{:S(2)}, u32[]{:S(2)}) %collective-permute-start.8) | collective-permute-done | bytes 65568 | tf_op jit(solution)/shard_map/ppermute | solution.py:43
  175.8 1.9 collective-permute-start.9
  177.8 7.0 %collective-permute-done.9 = bf16[4,128,128]{2,1,0:T(8,128)(2,1)S(1)} collective-permute-done((bf16[4,128,128]{2,1,0:T(8,128)(2,1)S(1)}, bf16[4,128,128]{2,1,0:T(8,128)(2,1)S(1)}, u32[]{:S(2)}, u32[]{:S(2)}) %collective-permute-start.9) | collective-permute-done | bytes 131104 | tf_op jit(solution)/shard_map/ppermute | solution.py:43
  184.8 1.9 collective-permute-start.10
  186.8 6.2 %collective-permute-done.10 = bf16[8,128,128]{2,1,0:T(8,128)(2,1)S(1)} collective-permute-done((bf16[8,128,128]{2,1,0:T(8,128)(2,1)S(1)}, bf16[8,128,128]{2,1,0:T(8,128)(2,1)S(1)}, u32[]{:S(2)}, u32[]{:S(2)}) %collective-permute-start.10) | collective-permute-done | bytes 262176 | tf_op jit(solution)/shard_map/ppermute | solution.py:43
  193.0 0.1 constant_dynamic-update-slice_fusion.5
  193.2 1.9 collective-permute-start.11
  195.1 0.1 fusion.18.index_ref
  195.2 1.8 collective-permute-done.11
  197.1 5.4 %place_rows.3 = bf16[4096,128]{1,0:T(8,128)(2,1)S(1)} custom-call(s32[4096]{0:T(1024)S(1)} %fusion.18.index_ref, bf16[4096,128]{1,0:T(8,128)(2,1)S(1)} %bitcast.35), custom_call_target="tpu_custom_call" | custom-call | bytes 6291456 | tf_op jit(solution)/shard_map/place_rows/pallas_call | solution.py:84
  202.4 0.4 fusion
  202.9 14.9 %all_to_all.31 = bf16[8,128,128]{2,1,0:T(8,128)(2,1)S(1)} all-to-all(bf16[8,128,128]{2,1,0:T(8,128)(2,1)S(1)} %broadcast_in_dim.52), channel_id=1, replica_groups={{0,64,128,192,256,320,384,448},{32,96,160,224,288,352,416,480},{512,576..., dimensions={0} | all-to-all | bytes 524288 | tf_op jit(solution)/shard_map/all_to_all | solution.py:27
  217.8 0.2 broadcast_in_dim.53
  218.0 18.2 %all_to_all.32 = bf16[4,8,128,128]{3,2,1,0:T(8,128)(2,1)} all-to-all(bf16[4,8,128,128]{3,2,1,0:T(8,128)(2,1)S(1)} %broadcast_in_dim.53), channel_id=1, replica_groups={{0,32,512,544},{64,96,576,608},{128,160,640,672},{192,224,704,736},{256..., dimensions={0} | all-to-all | bytes 2097152 | tf_op jit(solution)/shard_map/all_to_all | solution.py:31
  236.2 6.4 %apply_theta.1 = bf16[1024,128]{1,0:T(8,128)(2,1)} custom-call(bf16[1024,4096]{1,0:T(8,128)(2,1)} %theta_ref.1, bf16[4096,128]{1,0:T(8,128)(2,1)} %bitcast.41), custom_call_target="tpu_custom_call" | custom-call | flops 1073741824 | bytes 9437184 | tf_op jit(solution)/shard_map/apply_theta/pallas_call | solution.py:130
  (34 shorter events, 0.7 us)
Async XLA Ops:
  0.0 6.7 %copy-start = (bf16[1024,128]{1,0:T(8,128)(2,1)S(1)}, bf16[1024,128]{1,0:T(8,128)(2,1)}, u32[]{:S(2)}) copy-start(bf16[1024,128]{1,0:T(8,128)(2,1)} %param.5) | copy-start | bytes 786436
  37.0 17.9 %all-to-all-start.1 = ((bf16[4,8,128,128]{3,2,1,0:T(8,128)(2,1)}), bf16[4,8,128,128]{3,2,1,0:T(8,128)(2,1)S(1)}, u32[]{:S(2)}, u32[]{:S(2)}) async-start(bf16[4,8,128,128]{3,2,1,0:T(8,128)(2,1)} %broadcast_in_dim.26), calls=%async_computation.1 | async-start | bytes 2097152 | tf_op jit(solution)/shard_map/all_to_all | solution.py:31
  55.6 14.6 %copy-start.1 = (f32[128,128]{1,0:T(8,128)S(1)}, f32[128,128]{1,0:T(8,128)}, u32[]{:S(2)}) copy-start(f32[128,128]{1,0:T(8,128)} %param.8) | copy-start | bytes 196612
  57.0 67.1 %all-to-all-start.2 = ((bf16[32,128,128]{2,1,0:T(8,128)(2,1)}), bf16[32,128,128]{2,1,0:T(8,128)(2,1)S(1)}, u32[]{:S(2)}, u32[]{:S(2)}) async-start(bf16[32,128,128]{2,1,0:T(8,128)(2,1)} %bitcast.1), calls=%async_computation.2 | async-start | bytes 2097152 | tf_op jit(solution)/shard_map/all_to_all | solution.py:36
  70.2 25.5 %collective-permute-start = (bf16[128,128]{1,0:T(8,128)(2,1)S(1)}, bf16[128,128]{1,0:T(8,128)(2,1)S(1)}, u32[]{:S(2)}, u32[]{:S(2)}) collective-permute-start(bf16[128,128]{1,0:T(8,128)(2,1)S(1)} %get-tuple-element.12), channel_id=1, source_target_pairs={{0,8},{1,9},{2,10},{3,11},{4,12},{5,13},{6,14},{7,15},{8,0},{9,1},... | collective-permute-start | bytes 98312 | tf_op jit(solution)/shard_map/ppermute | solution.py:48
  74.5 26.6 %collective-permute-start.1 = (bf16[128,128]{1,0:T(8,128)(2,1)S(1)}, bf16[128,128]{1,0:T(8,128)(2,1)S(1)}, u32[]{:S(2)}, u32[]{:S(2)}) collective-permute-start(bf16[128,128]{1,0:T(8,128)(2,1)S(1)} %get-tuple-element.12), channel_id=1, source_target_pairs={{0,16},{1,17},{2,18},{3,19},{4,20},{5,21},{6,22},{7,23},{8,24},{9,... | collective-permute-start | bytes 98312 | tf_op jit(solution)/shard_map/ppermute | solution.py:48
  80.0 21.1 %collective-permute-start.2 = (bf16[128,128]{1,0:T(8,128)(2,1)S(1)}, bf16[128,128]{1,0:T(8,128)(2,1)S(1)}, u32[]{:S(2)}, u32[]{:S(2)}) collective-permute-start(bf16[128,128]{1,0:T(8,128)(2,1)S(1)} %get-tuple-element.12), channel_id=1, source_target_pairs={{0,24},{1,25},{2,26},{3,27},{4,28},{5,29},{6,30},{7,31},{8,16},{9,... | collective-permute-start | bytes 98312 | tf_op jit(solution)/shard_map/ppermute | solution.py:48
  101.1 13.8 %collective-permute-start.3 = (bf16[4,128,128]{2,1,0:T(8,128)(2,1)S(1)}, bf16[4,128,128]{2,1,0:T(8,128)(2,1)S(1)}, u32[]{:S(2)}, u32[]{:S(2)}) collective-permute-start(bf16[4,128,128]{2,1,0:T(8,128)(2,1)S(1)} %pad_maximum_fusion.1), channel_id=1, source_target_pairs={{0,4},{1,5},{2,6},{3,7},{4,0},{5,1},{6,2},{7,3},{8,12},{9,13},{10,... | collective-permute-start | bytes 393224 | tf_op jit(solution)/shard_map/ppermute | solution.py:48
  114.9 25.3 %collective-permute-start.4 = (bf16[8,128,128]{2,1,0:T(8,128)(2,1)S(1)}, bf16[8,128,128]{2,1,0:T(8,128)(2,1)S(1)}, u32[]{:S(2)}, u32[]{:S(2)}) collective-permute-start(bf16[8,128,128]{2,1,0:T(8,128)(2,1)S(1)} %constant_dynamic-update-slice_fusion.refs_0_), channel_id=1, source_target_pairs={{0,1},{1,0},{2,3},{3,2},{4,5},{5,4},{6,7},{7,6},{8,9},{9,8},{10,11... | collective-permute-start | bytes 786440 | tf_op jit(solution)/shard_map/ppermute | solution.py:48
  116.9 23.5 %collective-permute-start.5 = (bf16[8,128,128]{2,1,0:T(8,128)(2,1)S(1)}, bf16[8,128,128]{2,1,0:T(8,128)(2,1)S(1)}, u32[]{:S(2)}, u32[]{:S(2)}) collective-permute-start(bf16[8,128,128]{2,1,0:T(8,128)(2,1)S(1)} %constant_dynamic-update-slice_fusion.refs_0_), channel_id=1, source_target_pairs={{0,2},{1,3},{2,0},{3,1},{4,6},{5,7},{6,4},{7,5},{8,10},{9,11},{10,... | collective-permute-start | bytes 786440 | tf_op jit(solution)/shard_map/ppermute | solution.py:48
  119.3 39.3 %collective-permute-start.6 = (bf16[8,128,128]{2,1,0:T(8,128)(2,1)S(1)}, bf16[8,128,128]{2,1,0:T(8,128)(2,1)S(1)}, u32[]{:S(2)}, u32[]{:S(2)}) collective-permute-start(bf16[8,128,128]{2,1,0:T(8,128)(2,1)S(1)} %constant_dynamic-update-slice_fusion.refs_0_), channel_id=1, source_target_pairs={{0,3},{1,2},{2,1},{3,0},{4,7},{5,6},{6,5},{7,4},{8,11},{9,10},{10,... | collective-permute-start | bytes 786440 | tf_op jit(solution)/shard_map/ppermute | solution.py:48
  125.7 76.7 %all-to-all-start.3 = ((bf16[32,128,128]{1,2,0:T(8,128)(2,1)}), bf16[32,128,128]{1,2,0:T(8,128)(2,1)S(1)}, u32[]{:S(2)}, u32[]{:S(2)}) async-start(bf16[32,128,128]{1,2,0:T(8,128)(2,1)} %broadcast_in_dim.49), calls=%async_computation.3 | async-start | bytes 2097152 | tf_op jit(solution)/shard_map/all_to_all | solution.py:36
  159.0 6.1 %collective-permute-start.7 = (bf16[1,128,128]{2,1,0:T(8,128)(2,1)S(1)}, bf16[1,128,128]{2,1,0:T(8,128)(2,1)S(1)}, u32[]{:S(2)}, u32[]{:S(2)}) collective-permute-start(bf16[1,128,128]{2,1,0:T(8,128)(2,1)S(1)} %bitcast.36), channel_id=1, source_target_pairs={{0,512},{32,544},{64,576},{96,608},{128,640},{160,672},{192,704},{... | collective-permute-start | bytes 98312 | tf_op jit(solution)/shard_map/ppermute | solution.py:43
  165.1 10.7 %collective-permute-start.8 = (bf16[2,128,128]{2,1,0:T(8,128)(2,1)S(1)}, bf16[2,128,128]{2,1,0:T(8,128)(2,1)S(1)}, u32[]{:S(2)}, u32[]{:S(2)}) collective-permute-start(bf16[2,128,128]{2,1,0:T(8,128)(2,1)S(1)} %pad_maximum_fusion.3), channel_id=1, source_target_pairs={{0,256},{32,288},{64,320},{96,352},{128,384},{160,416},{192,448},{... | collective-permute-start | bytes 196616 | tf_op jit(solution)/shard_map/ppermute | solution.py:43
  175.8 8.9 %collective-permute-start.9 = (bf16[4,128,128]{2,1,0:T(8,128)(2,1)S(1)}, bf16[4,128,128]{2,1,0:T(8,128)(2,1)S(1)}, u32[]{:S(2)}, u32[]{:S(2)}) collective-permute-start(bf16[4,128,128]{2,1,0:T(8,128)(2,1)S(1)} %pad_maximum_fusion.2), channel_id=1, source_target_pairs={{0,128},{32,160},{64,192},{96,224},{128,0},{160,32},{192,64},{224,... | collective-permute-start | bytes 393224 | tf_op jit(solution)/shard_map/ppermute | solution.py:43
  184.8 8.3 %collective-permute-start.10 = (bf16[8,128,128]{2,1,0:T(8,128)(2,1)S(1)}, bf16[8,128,128]{2,1,0:T(8,128)(2,1)S(1)}, u32[]{:S(2)}, u32[]{:S(2)}) collective-permute-start(bf16[8,128,128]{2,1,0:T(8,128)(2,1)S(1)} %pad_maximum_fusion), channel_id=1, source_target_pairs={{0,64},{32,96},{64,0},{96,32},{128,192},{160,224},{192,128},{224,1... | collective-permute-start | bytes 786440 | tf_op jit(solution)/shard_map/ppermute | solution.py:43
  193.2 3.8 %collective-permute-start.11 = (bf16[16,128,128]{2,1,0:T(8,128)(2,1)S(1)}, bf16[16,128,128]{2,1,0:T(8,128)(2,1)S(1)}, u32[]{:S(2)}, u32[]{:S(2)}) collective-permute-start(bf16[16,128,128]{2,1,0:T(8,128)(2,1)S(1)} %get-tuple-element.13), channel_id=1, source_target_pairs={{0,32},{32,0},{64,96},{96,64},{128,160},{160,128},{192,224},{224,1... | collective-permute-start | bytes 1572872 | tf_op jit(solution)/shard_map/ppermute | solution.py:43

commit v5 on v4

--- a/solution.py
+++ b/solution.py
@@ -63,7 +63,6 @@
 
 
 ROWS_A_STEP = 16
-ROWS_A_DOT = 256
 IN_VMEM = pl.BlockSpec(memory_space=pltpu.VMEM)
 
 
@@ -119,28 +118,55 @@
     )(*parts, rows)
 
 
-def apply_kernel(theta_ref, coeffs_ref, applied_ref):
-    applied_ref[...] = jnp.dot(
-        theta_ref[...], coeffs_ref[...], preferred_element_type=jnp.float32
-    ).astype(applied_ref.dtype)
-
-
-def apply(theta, coeffs):
-    rows, depth, columns = *theta.shape, coeffs.shape[1]
+BLOCKS_A_STEP = 4
+
+
+def apply_kernel(_, *refs):
+    *theta_refs, part_ref, total_ref, applied_ref, total = refs
+
+    @pl.when(pl.program_id(0) == 0)
+    def _():
+        total[...] = total_ref[...]
+
+    theta = jnp.concatenate([ref[...] for ref in theta_refs], axis=1)
+    part = part_ref[pl.ds(pl.program_id(0) * BLOCKS_A_STEP, BLOCKS_A_STEP)]
+    part = part.reshape(theta.shape[1], part_ref.shape[2])
+    total[...] += jnp.dot(theta, part, preferred_element_type=jnp.float32)
+
+    @pl.when(pl.program_id(0) == pl.num_programs(0) - 1)
+    def _():
+        applied_ref[...] = total[...].astype(applied_ref.dtype)
+
+
+def apply(theta, part, first, total, dtype):
+    rows = theta.shape[0]
+    blocks, own, columns = part.shape
+    if total is None:
+        total = jnp.zeros((rows, columns), jnp.float32)
+
+    def theta_spec(k):
+        return pl.BlockSpec((rows, own), lambda i, first_ref: (0, first_ref[0] + (i * BLOCKS_A_STEP + k) * CORE))
+
     return pl.pallas_call(
         apply_kernel,
-        out_shape=jax.ShapeDtypeStruct((rows, columns), theta.dtype),
-        grid=(rows // ROWS_A_DOT,),
-        in_specs=[
-            pl.BlockSpec((ROWS_A_DOT, depth), lambda i: (i, 0)),
-            pl.BlockSpec((depth, columns), lambda i: (0, 0), pipeline_mode=pl.Buffered(1)),
-        ],
-        out_specs=pl.BlockSpec((ROWS_A_DOT, columns), lambda i: (i, 0)),
+        out_shape=jax.ShapeDtypeStruct((rows, columns), dtype),
+        grid_spec=pltpu.PrefetchScalarGridSpec(
+            num_scalar_prefetch=1,
+            grid=(blocks // BLOCKS_A_STEP,),
+            in_specs=[
+                *(theta_spec(k) for k in range(BLOCKS_A_STEP)),
+                IN_VMEM,
+                IN_VMEM,
+            ],
+            out_specs=IN_VMEM,
+            scratch_shapes=[pltpu.VMEM((rows, columns), jnp.float32)],
+        ),
+        compiler_params=pltpu.CompilerParams(vmem_limit_bytes=50 << 20),
         cost_estimate=pl.CostEstimate(
-            flops=2 * rows * depth * columns, bytes_accessed=2 * (theta.size + coeffs.size), transcendentals=0
+            flops=2 * rows * part.size, bytes_accessed=2 * rows * blocks * own, transcendentals=0
         ),
         name="apply_theta",
-    )(theta, coeffs)
+    )(first.reshape(1), *([theta] * BLOCKS_A_STEP), part, total)
 
 
 def take(rows, index):
@@ -163,8 +189,7 @@
     placing = lax.sort_key_val(order, slots)[1]
     placing = in_gather_order(placing // own) * own + placing % own
 
-    mine = in_gather_order(me)
-    my_points = take(gathered, lax.dynamic_slice_in_dim(placing, mine * own, own, 0))
+    my_points = take(gathered, lax.dynamic_slice_in_dim(placing, me * own, own, 0))
     partial_rows = lax.dot_general(
         gathered, my_points, (((1,), (1,)), ((), ())), preferred_element_type=jnp.float32
     ).astype(jnp.bfloat16)
@@ -185,8 +210,21 @@
         (((0, 1), (0, 1)), ((), ())),
         preferred_element_type=jnp.float32,
     ).astype(jnp.bfloat16)
-    coeffs = gather_yc(gather_z(coeffs)).reshape(point_count, -1)
-    return apply(theta, coeffs)
+    coeffs = gather_z(coeffs)
+    other_y = swap(coeffs, "grid", Z * CORE)
+    other_core = swap(coeffs, "grid", 1)
+    other_both = swap(other_y, "grid", 1)
+    first = me // (Z * CORE) * (Z * CORE) + me % CORE
+    total = None
+    for name, part, bits in (
+        ("own", coeffs, 0),
+        ("core", other_core, 1),
+        ("y", other_y, Z * CORE),
+        ("both", other_both, Z * CORE + 1),
+    ):
+        dtype = jnp.bfloat16 if name == "both" else jnp.float32
+        total = apply(theta, part, first ^ bits, total, dtype)
+    return total
 
 
 def solution(mesh):

time: 244 us -> 241 us (0.988)
  the two profiles are of different devices: /device:TPU:4 before, /device:TPU:13 now
where the time goes in v5:
time: 241 us; the launch traced here: 240 us
  starting transfers between devices  80.8 us (34%)
  waiting for transfers between devices  76.9 us (32%)
  blocking collectives  41.4 us (17%)
  Pallas kernels  20.8 us (9%)
  other arithmetic  12.9 us (5%)
  local copies, waits for them, and re-layouts  5.1 us (2%)
    ppermute x10, waiting for transfers between devices, swap(): lax.ppermute(x, axis, [(i, i ^ bit) for i in range(lax.axis_size(axis))])  42.8 us
    all_to_all x2, blocking collectives, gather_z(): lax.all_to_all(spread(x, Z), 'grid', 0, 0, axis_index_groups=Z_GROUPS, ti...  41.4 us
    ppermute x10, starting transfers between devices, swap(): lax.ppermute(x, axis, [(i, i ^ bit) for i in range(lax.axis_size(axis))])  35.5 us
    ppermute x5, waiting for transfers between devices, gather_doubling(): lax.ppermute(x, axis, [(j, j ^ bit) for j in range(count)])  26.5 us
    all_to_all x2, starting transfers between devices, exchange_band(): return lax.all_to_all(blocks, 'band', 0, 0, tiled=True)  21.4 us
    ppermute x5, starting transfers between devices, gather_doubling(): lax.ppermute(x, axis, [(j, j ^ bit) for j in range(count)])  18.1 us
    pallas_call x2, Pallas kernels, place(): pl.pallas_call(place_kernel, out_shape=jax.ShapeDtypeStruct(rows.shape, r...  10.7 us
    pallas_call x4, Pallas kernels, apply(): pl.pallas_call(apply_kernel, out_shape=jax.ShapeDtypeStruct((rows, column...  9.71 us
  transfers between devices with their start and end apart: 18, of which 11 were waited for; matrix products, arithmetic and copies ran while one was open for 4% of the time, Pallas kernels for 7%

profile of v5, /device:TPU:13, one launch (start us, length us, event | category | flops | bytes accessed | tf_op | source)
XLA Modules:
  0.0 240.3 jit_solution(13065223789637501894)
XLA Ops:
  0.0 0.7 broadcast_xor_fusion
  0.7 5.9 %sort.30 = (s32[4096]{0:T(1024)S(1)}, s32[4096]{0:T(1024)S(1)}) sort(s32[4096]{0:T(1024)} %param.6, s32[4096]{0:T(1024)S(1)} %iota.5), dimensions={0}, to_apply=%region_0.0 | sort | flops 49152 | bytes 65536 | tf_op jit(solution)/shard_map/sort | solution.py:183
  6.7 0.7 gather_fusion
  7.4 26.7 %all_to_all.25 = bf16[8,128,128]{2,1,0:T(8,128)(2,1)S(1)} all-to-all(bf16[8,128,128]{2,1,0:T(8,128)(2,1)S(1)} %broadcast_in_dim.43), channel_id=1, replica_groups={{0,64,128,192,256,320,384,448},{32,96,160,224,288,352,416,480},{512,576..., dimensions={0} | all-to-all | bytes 524288 | tf_op jit(solution)/shard_map/all_to_all | solution.py:27
  34.1 1.2 broadcast_in_dim.44
  35.4 5.8 %all-to-all-start.1 = ((bf16[4,8,128,128]{3,2,1,0:T(8,128)(2,1)}), bf16[4,8,128,128]{3,2,1,0:T(8,128)(2,1)S(1)}, u32[]{:S(2)}, u32[]{:S(2)}) async-start(bf16[4,8,128,128]{3,2,1,0:T(8,128)(2,1)} %broadcast_in_dim.44), calls=%async_computation.1 | async-start | bytes 2097152 | tf_op jit(solution)/shard_map/all_to_all | solution.py:31
  41.2 5.8 %sort.31 = (s32[4096]{0:T(1024)}, s32[4096]{0:T(1024)S(1)}) sort(s32[4096]{0:T(1024)S(1)} %get-tuple-element.9, s32[4096]{0:T(1024)S(1)} %iota.6), dimensions={0}, to_apply=%region_1.2 | sort | flops 49152 | bytes 65536 | tf_op jit(solution)/shard_map/sort | solution.py:189
  47.1 7.5 %all-to-all-done.1 = bf16[4,8,128,128]{3,2,1,0:T(8,128)(2,1)S(1)} async-done(((bf16[4,8,128,128]{3,2,1,0:T(8,128)(2,1)}), bf16[4,8,128,128]{3,2,1,0:T(8,128)(2,1)S(1)}, u32[]{:S(2)}, u32[]{:S(2)}) %all-to-all-start.1) | async-done | bytes 1048608 | tf_op jit(solution)/shard_map/all_to_all | solution.py:31
  54.6 0.7 gather_fusion.1
  55.4 1.4 convolution_convert_fusion
  56.8 12.5 %all-to-all-start.2 = ((bf16[32,128,128]{2,1,0:T(8,128)(2,1)}), bf16[32,128,128]{2,1,0:T(8,128)(2,1)S(1)}, u32[]{:S(2)}, u32[]{:S(2)}) async-start(bf16[32,128,128]{2,1,0:T(8,128)(2,1)} %bitcast.2), calls=%async_computation.2 | async-start | bytes 2097152 | tf_op jit(solution)/shard_map/all_to_all | solution.py:36
  69.3 4.0 %collective-permute-start = (bf16[128,128]{1,0:T(8,128)(2,1)S(1)}, bf16[128,128]{1,0:T(8,128)(2,1)S(1)}, u32[]{:S(2)}, u32[]{:S(2)}) collective-permute-start(bf16[128,128]{1,0:T(8,128)(2,1)S(1)} %get-tuple-element.12), channel_id=1, source_target_pairs={{0,8},{1,9},{2,10},{3,11},{4,12},{5,13},{6,14},{7,15},{8,0},{9,1},... | collective-permute-start | bytes 98312 | tf_op jit(solution)/shard_map/ppermute | solution.py:48
  73.3 5.3 %collective-permute-start.1 = (bf16[128,128]{1,0:T(8,128)(2,1)S(1)}, bf16[128,128]{1,0:T(8,128)(2,1)S(1)}, u32[]{:S(2)}, u32[]{:S(2)}) collective-permute-start(bf16[128,128]{1,0:T(8,128)(2,1)S(1)} %get-tuple-element.12), channel_id=1, source_target_pairs={{0,16},{1,17},{2,18},{3,19},{4,20},{5,21},{6,22},{7,23},{8,24},{9,... | collective-permute-start | bytes 98312 | tf_op jit(solution)/shard_map/ppermute | solution.py:48
  78.6 2.1 collective-permute-start.2
  80.7 16.6 %collective-permute-done = bf16[128,128]{1,0:T(8,128)(2,1)S(1)} collective-permute-done((bf16[128,128]{1,0:T(8,128)(2,1)S(1)}, bf16[128,128]{1,0:T(8,128)(2,1)S(1)}, u32[]{:S(2)}, u32[]{:S(2)}) %collective-permute-start) | collective-permute-done | bytes 32800 | tf_op jit(solution)/shard_map/ppermute | solution.py:48
  97.3 2.3 collective-permute-done.1
  99.6 5.3 %collective-permute-start.3 = (bf16[4,128,128]{2,1,0:T(8,128)(2,1)S(1)}, bf16[4,128,128]{2,1,0:T(8,128)(2,1)S(1)}, u32[]{:S(2)}, u32[]{:S(2)}) collective-permute-start(bf16[4,128,128]{2,1,0:T(8,128)(2,1)S(1)} %pad_maximum_fusion.1), channel_id=1, source_target_pairs={{0,4},{1,5},{2,6},{3,7},{4,0},{5,1},{6,2},{7,3},{8,12},{9,13},{10,... | collective-permute-start | bytes 393224 | tf_op jit(solution)/shard_map/ppermute | solution.py:48
  105.0 4.9 %collective-permute-done.3 = bf16[4,128,128]{2,1,0:T(8,128)(2,1)S(1)} collective-permute-done((bf16[4,128,128]{2,1,0:T(8,128)(2,1)S(1)}, bf16[4,128,128]{2,1,0:T(8,128)(2,1)S(1)}, u32[]{:S(2)}, u32[]{:S(2)}) %collective-permute-start.3) | collective-permute-done | bytes 131104 | tf_op jit(solution)/shard_map/ppermute | solution.py:48
  109.9 5.2 %collective-permute-start.4 = (bf16[8,128,128]{2,1,0:T(8,128)(2,1)S(1)}, bf16[8,128,128]{2,1,0:T(8,128)(2,1)S(1)}, u32[]{:S(2)}, u32[]{:S(2)}) collective-permute-start(bf16[8,128,128]{2,1,0:T(8,128)(2,1)S(1)} %constant_dynamic-update-slice_fusion.refs_0_), channel_id=1, source_target_pairs={{0,1},{1,0},{2,3},{3,2},{4,5},{5,4},{6,7},{7,6},{8,9},{9,8},{10,11... | collective-permute-start | bytes 786440 | tf_op jit(solution)/shard_map/ppermute | solution.py:48
  115.1 3.8 %collective-permute-start.5 = (bf16[8,128,128]{2,1,0:T(8,128)(2,1)S(1)}, bf16[8,128,128]{2,1,0:T(8,128)(2,1)S(1)}, u32[]{:S(2)}, u32[]{:S(2)}) collective-permute-start(bf16[8,128,128]{2,1,0:T(8,128)(2,1)S(1)} %constant_dynamic-update-slice_fusion.refs_0_), channel_id=1, source_target_pairs={{0,2},{1,3},{2,0},{3,1},{4,6},{5,7},{6,4},{7,5},{8,10},{9,11},{10,... | collective-permute-start | bytes 786440 | tf_op jit(solution)/shard_map/ppermute | solution.py:48
  119.0 2.2 collective-permute-start.6
  121.5 1.2 broadcast_in_dim.46
  122.7 8.9 %all-to-all-start.3 = ((bf16[32,128,128]{1,2,0:T(8,128)(2,1)}), bf16[32,128,128]{1,2,0:T(8,128)(2,1)S(1)}, u32[]{:S(2)}, u32[]{:S(2)}) async-start(bf16[32,128,128]{1,2,0:T(8,128)(2,1)} %broadcast_in_dim.46), calls=%async_computation.3 | async-start | bytes 2097152 | tf_op jit(solution)/shard_map/all_to_all | solution.py:36
  131.7 0.6 gather_fusion.2
  132.2 5.4 %place_rows.2.refs_4_ = bf16[4096,128]{1,0:T(8,128)(2,1)S(1)} custom-call(s32[4096]{0:T(1024)S(1)} %bitcast.43, bf16[4096,128]{1,0:T(8,128)(2,1)S(1)} %bitcast.36), custom_call_target="tpu_custom_call" | custom-call | bytes 6291456 | tf_op jit(solution)/shard_map/place_rows/pallas_call | solution.py:83
  137.6 14.1 %collective-permute-done.6.refs_3_ = bf16[8,128,128]{2,1,0:T(8,128)(2,1)S(1)} collective-permute-done((bf16[8,128,128]{2,1,0:T(8,128)(2,1)S(1)}, bf16[8,128,128]{2,1,0:T(8,128)(2,1)S(1)}, u32[]{:S(2)}, u32[]{:S(2)}) %collective-permute-start.6) | collective-permute-done | bytes 262176 | tf_op jit(solution)/shard_map/ppermute | solution.py:48
  151.8 0.4 multiply_metric.1
  152.2 1.9 collective-permute-start.7
  154.1 5.9 %collective-permute-done.7 = bf16[1,128,128]{2,1,0:T(8,128)(2,1)S(1)} collective-permute-done((bf16[1,128,128]{2,1,0:T(8,128)(2,1)S(1)}, bf16[1,128,128]{2,1,0:T(8,128)(2,1)S(1)}, u32[]{:S(2)}, u32[]{:S(2)}) %collective-permute-start.7) | collective-permute-done | bytes 32800 | tf_op jit(solution)/shard_map/ppermute | solution.py:43
  160.1 1.9 collective-permute-start.8
  162.0 7.0 %collective-permute-done.8 = bf16[2,128,128]{2,1,0:T(8,128)(2,1)S(1)} collective-permute-done((bf16[2,128,128]{2,1,0:T(8,128)(2,1)S(1)}, bf16[2,128,128]{2,1,0:T(8,128)(2,1)S(1)}, u32[]{:S(2)}, u32[]{:S(2)}) %collective-permute-start.8) | collective-permute-done | bytes 65568 | tf_op jit(solution)/shard_map/ppermute | solution.py:43
  169.0 1.9 collective-permute-start.9
  170.9 5.7 %collective-permute-done.9 = bf16[4,128,128]{2,1,0:T(8,128)(2,1)S(1)} collective-permute-done((bf16[4,128,128]{2,1,0:T(8,128)(2,1)S(1)}, bf16[4,128,128]{2,1,0:T(8,128)(2,1)S(1)}, u32[]{:S(2)}, u32[]{:S(2)}) %collective-permute-start.9) | collective-permute-done | bytes 131104 | tf_op jit(solution)/shard_map/ppermute | solution.py:43
  176.7 1.9 collective-permute-start.10
  178.7 6.5 %collective-permute-done.10 = bf16[8,128,128]{2,1,0:T(8,128)(2,1)S(1)} collective-permute-done((bf16[8,128,128]{2,1,0:T(8,128)(2,1)S(1)}, bf16[8,128,128]{2,1,0:T(8,128)(2,1)S(1)}, u32[]{:S(2)}, u32[]{:S(2)}) %collective-permute-start.10) | collective-permute-done | bytes 262176 | tf_op jit(solution)/shard_map/ppermute | solution.py:43
  185.4 10.4 %collective-permute-start.11 = (bf16[16,128,128]{2,1,0:T(8,128)(2,1)S(1)}, bf16[16,128,128]{2,1,0:T(8,128)(2,1)S(1)}, u32[]{:S(2)}, u32[]{:S(2)}) collective-permute-start(bf16[16,128,128]{2,1,0:T(8,128)(2,1)S(1)} %get-tuple-element.13), channel_id=1, source_target_pairs={{0,32},{32,0},{64,96},{96,64},{128,160},{160,128},{192,224},{224,1... | collective-permute-start | bytes 1572872 | tf_op jit(solution)/shard_map/ppermute | solution.py:43
  195.9 1.4 collective-permute-done.11
  197.4 5.4 %place_rows.3 = bf16[4096,128]{1,0:T(8,128)(2,1)S(1)} custom-call(s32[4096]{0:T(1024)S(1)} %fusion.18.index_ref, bf16[4096,128]{1,0:T(8,128)(2,1)S(1)} %bitcast.38), custom_call_target="tpu_custom_call" | custom-call | bytes 6291456 | tf_op jit(solution)/shard_map/place_rows/pallas_call | solution.py:83
  202.8 0.4 fusion
  203.2 14.7 %all_to_all.26.refs_4_ = bf16[8,128,128]{2,1,0:T(8,128)(2,1)S(1)} all-to-all(bf16[8,128,128]{2,1,0:T(8,128)(2,1)S(1)} %broadcast_in_dim.49), channel_id=1, replica_groups={{0,64,128,192,256,320,384,448},{32,96,160,224,288,352,416,480},{512,576..., dimensions={0} | all-to-all | bytes 524288 | tf_op jit(solution)/shard_map/all_to_all | solution.py:27
  217.9 1.9 collective-permute-start.12
  219.9 2.4 %collective-permute-start.14 = (bf16[8,128,128]{2,1,0:T(8,128)(2,1)S(1)}, bf16[8,128,128]{2,1,0:T(8,128)(2,1)S(1)}, u32[]{:S(2)}, u32[]{:S(2)}) collective-permute-start(bf16[8,128,128]{2,1,0:T(8,128)(2,1)S(1)} %all_to_all.26.refs_4_), channel_id=1, source_target_pairs={{0,32},{32,0},{64,96},{96,64},{128,160},{160,128},{192,224},{224,1... | collective-permute-start | bytes 786440 | tf_op jit(solution)/shard_map/ppermute | solution.py:48
  222.3 4.9 %collective-permute-done.12.refs_4_ = bf16[8,128,128]{2,1,0:T(8,128)(2,1)S(1)} collective-permute-done((bf16[8,128,128]{2,1,0:T(8,128)(2,1)S(1)}, bf16[8,128,128]{2,1,0:T(8,128)(2,1)S(1)}, u32[]{:S(2)}, u32[]{:S(2)}) %collective-permute-start.12) | collective-permute-done | bytes 262176 | tf_op jit(solution)/shard_map/ppermute | solution.py:48
  227.2 3.3 %collective-permute-start.13 = (bf16[8,128,128]{2,1,0:T(8,128)(2,1)S(1)}, bf16[8,128,128]{2,1,0:T(8,128)(2,1)S(1)}, u32[]{:S(2)}, u32[]{:S(2)}) collective-permute-start(bf16[8,128,128]{2,1,0:T(8,128)(2,1)S(1)} %collective-permute-done.12.refs_4_), channel_id=1, source_target_pairs={{0,32},{32,0},{64,96},{96,64},{128,160},{160,128},{192,224},{224,1... | collective-permute-start | bytes 786440 | tf_op jit(solution)/shard_map/ppermute | solution.py:48
  230.5 2.3 apply_theta.4.refs_5_
  232.8 2.3 apply_theta.5.refs_5_
  235.1 2.3 apply_theta.6.refs_5_
  237.4 2.9 %apply_theta.7 = bf16[1024,128]{1,0:T(8,128)(2,1)} custom-call(s32[1]{0:T(128)} %bitcast._, bf16[1024,4096]{1,0:T(8,128)(2,1)} %refs_3_.7, bf16[1024,4096]{1,0:T(8,128)(2,1)} %refs_3_.7, bf16[1024,4096]{1,0:T(8,128)(2,1)} %refs_3_.7, bf16[1024,4096]{1,0:T(8,128)(2,1)} %refs_3_.7, bf16[8,128,128]{2,1,0:T(8,128)(2,1)S(1)} %collective-permute-done.13.refs_4_, ...), custom_call_target="tpu_custom_call" | custom-call | flops 268435456 | bytes 2097152 | tf_op jit(solution)/shard_map/apply_theta/pallas_call | solution.py:150
  (42 shorter events, 1.2 us)
Async XLA Ops:
  0.0 6.7 %copy-start = (bf16[1024,128]{1,0:T(8,128)(2,1)S(1)}, bf16[1024,128]{1,0:T(8,128)(2,1)}, u32[]{:S(2)}) copy-start(bf16[1024,128]{1,0:T(8,128)(2,1)} %param.5) | copy-start | bytes 786436
  35.4 19.3 %all-to-all-start.1 = ((bf16[4,8,128,128]{3,2,1,0:T(8,128)(2,1)}), bf16[4,8,128,128]{3,2,1,0:T(8,128)(2,1)S(1)}, u32[]{:S(2)}, u32[]{:S(2)}) async-start(bf16[4,8,128,128]{3,2,1,0:T(8,128)(2,1)} %broadcast_in_dim.44), calls=%async_computation.1 | async-start | bytes 2097152 | tf_op jit(solution)/shard_map/all_to_all | solution.py:31
  55.4 13.9 %copy-start.1 = (f32[128,128]{1,0:T(8,128)S(1)}, f32[128,128]{1,0:T(8,128)}, u32[]{:S(2)}) copy-start(f32[128,128]{1,0:T(8,128)} %param.8) | copy-start | bytes 196612
  56.8 64.4 %all-to-all-start.2 = ((bf16[32,128,128]{2,1,0:T(8,128)(2,1)}), bf16[32,128,128]{2,1,0:T(8,128)(2,1)S(1)}, u32[]{:S(2)}, u32[]{:S(2)}) async-start(bf16[32,128,128]{2,1,0:T(8,128)(2,1)} %bitcast.2), calls=%async_computation.2 | async-start | bytes 2097152 | tf_op jit(solution)/shard_map/all_to_all | solution.py:36
  69.3 28.0 %collective-permute-start = (bf16[128,128]{1,0:T(8,128)(2,1)S(1)}, bf16[128,128]{1,0:T(8,128)(2,1)S(1)}, u32[]{:S(2)}, u32[]{:S(2)}) collective-permute-start(bf16[128,128]{1,0:T(8,128)(2,1)S(1)} %get-tuple-element.12), channel_id=1, source_target_pairs={{0,8},{1,9},{2,10},{3,11},{4,12},{5,13},{6,14},{7,15},{8,0},{9,1},... | collective-permute-start | bytes 98312 | tf_op jit(solution)/shard_map/ppermute | solution.py:48
  73.3 26.3 %collective-permute-start.1 = (bf16[128,128]{1,0:T(8,128)(2,1)S(1)}, bf16[128,128]{1,0:T(8,128)(2,1)S(1)}, u32[]{:S(2)}, u32[]{:S(2)}) collective-permute-start(bf16[128,128]{1,0:T(8,128)(2,1)S(1)} %get-tuple-element.12), channel_id=1, source_target_pairs={{0,16},{1,17},{2,18},{3,19},{4,20},{5,21},{6,22},{7,23},{8,24},{9,... | collective-permute-start | bytes 98312 | tf_op jit(solution)/shard_map/ppermute | solution.py:48
  78.6 21.0 %collective-permute-start.2 = (bf16[128,128]{1,0:T(8,128)(2,1)S(1)}, bf16[128,128]{1,0:T(8,128)(2,1)S(1)}, u32[]{:S(2)}, u32[]{:S(2)}) collective-permute-start(bf16[128,128]{1,0:T(8,128)(2,1)S(1)} %get-tuple-element.12), channel_id=1, source_target_pairs={{0,24},{1,25},{2,26},{3,27},{4,28},{5,29},{6,30},{7,31},{8,16},{9,... | collective-permute-start | bytes 98312 | tf_op jit(solution)/shard_map/ppermute | solution.py:48
  99.6 10.3 %collective-permute-start.3 = (bf16[4,128,128]{2,1,0:T(8,128)(2,1)S(1)}, bf16[4,128,128]{2,1,0:T(8,128)(2,1)S(1)}, u32[]{:S(2)}, u32[]{:S(2)}) collective-permute-start(bf16[4,128,128]{2,1,0:T(8,128)(2,1)S(1)} %pad_maximum_fusion.1), channel_id=1, source_target_pairs={{0,4},{1,5},{2,6},{3,7},{4,0},{5,1},{6,2},{7,3},{8,12},{9,13},{10,... | collective-permute-start | bytes 393224 | tf_op jit(solution)/shard_map/ppermute | solution.py:48
  109.9 27.7 %collective-permute-start.4 = (bf16[8,128,128]{2,1,0:T(8,128)(2,1)S(1)}, bf16[8,128,128]{2,1,0:T(8,128)(2,1)S(1)}, u32[]{:S(2)}, u32[]{:S(2)}) collective-permute-start(bf16[8,128,128]{2,1,0:T(8,128)(2,1)S(1)} %constant_dynamic-update-slice_fusion.refs_0_), channel_id=1, source_target_pairs={{0,1},{1,0},{2,3},{3,2},{4,5},{5,4},{6,7},{7,6},{8,9},{9,8},{10,11... | collective-permute-start | bytes 786440 | tf_op jit(solution)/shard_map/ppermute | solution.py:48
  115.1 22.5 %collective-permute-start.5 = (bf16[8,128,128]{2,1,0:T(8,128)(2,1)S(1)}, bf16[8,128,128]{2,1,0:T(8,128)(2,1)S(1)}, u32[]{:S(2)}, u32[]{:S(2)}) collective-permute-start(bf16[8,128,128]{2,1,0:T(8,128)(2,1)S(1)} %constant_dynamic-update-slice_fusion.refs_0_), channel_id=1, source_target_pairs={{0,2},{1,3},{2,0},{3,1},{4,6},{5,7},{6,4},{7,5},{8,10},{9,11},{10,... | collective-permute-start | bytes 786440 | tf_op jit(solution)/shard_map/ppermute | solution.py:48
  119.0 32.8 %collective-permute-start.6 = (bf16[8,128,128]{2,1,0:T(8,128)(2,1)S(1)}, bf16[8,128,128]{2,1,0:T(8,128)(2,1)S(1)}, u32[]{:S(2)}, u32[]{:S(2)}) collective-permute-start(bf16[8,128,128]{2,1,0:T(8,128)(2,1)S(1)} %constant_dynamic-update-slice_fusion.refs_0_), channel_id=1, source_target_pairs={{0,3},{1,2},{2,1},{3,0},{4,7},{5,6},{6,5},{7,4},{8,11},{9,10},{10,... | collective-permute-start | bytes 786440 | tf_op jit(solution)/shard_map/ppermute | solution.py:48
  122.7 80.1 %all-to-all-start.3 = ((bf16[32,128,128]{1,2,0:T(8,128)(2,1)}), bf16[32,128,128]{1,2,0:T(8,128)(2,1)S(1)}, u32[]{:S(2)}, u32[]{:S(2)}) async-start(bf16[32,128,128]{1,2,0:T(8,128)(2,1)} %broadcast_in_dim.46), calls=%async_computation.3 | async-start | bytes 2097152 | tf_op jit(solution)/shard_map/all_to_all | solution.py:36
  152.2 7.8 %collective-permute-start.7 = (bf16[1,128,128]{2,1,0:T(8,128)(2,1)S(1)}, bf16[1,128,128]{2,1,0:T(8,128)(2,1)S(1)}, u32[]{:S(2)}, u32[]{:S(2)}) collective-permute-start(bf16[1,128,128]{2,1,0:T(8,128)(2,1)S(1)} %bitcast.39), channel_id=1, source_target_pairs={{0,512},{32,544},{64,576},{96,608},{128,640},{160,672},{192,704},{... | collective-permute-start | bytes 98312 | tf_op jit(solution)/shard_map/ppermute | solution.py:43
  160.1 8.9 %collective-permute-start.8 = (bf16[2,128,128]{2,1,0:T(8,128)(2,1)S(1)}, bf16[2,128,128]{2,1,0:T(8,128)(2,1)S(1)}, u32[]{:S(2)}, u32[]{:S(2)}) collective-permute-start(bf16[2,128,128]{2,1,0:T(8,128)(2,1)S(1)} %pad_maximum_fusion.3), channel_id=1, source_target_pairs={{0,256},{32,288},{64,320},{96,352},{128,384},{160,416},{192,448},{... | collective-permute-start | bytes 196616 | tf_op jit(solution)/shard_map/ppermute | solution.py:43
  169.0 7.7 %collective-permute-start.9 = (bf16[4,128,128]{2,1,0:T(8,128)(2,1)S(1)}, bf16[4,128,128]{2,1,0:T(8,128)(2,1)S(1)}, u32[]{:S(2)}, u32[]{:S(2)}) collective-permute-start(bf16[4,128,128]{2,1,0:T(8,128)(2,1)S(1)} %pad_maximum_fusion.2), channel_id=1, source_target_pairs={{0,128},{32,160},{64,192},{96,224},{128,0},{160,32},{192,64},{224,... | collective-permute-start | bytes 393224 | tf_op jit(solution)/shard_map/ppermute | solution.py:43
  176.7 8.5 %collective-permute-start.10 = (bf16[8,128,128]{2,1,0:T(8,128)(2,1)S(1)}, bf16[8,128,128]{2,1,0:T(8,128)(2,1)S(1)}, u32[]{:S(2)}, u32[]{:S(2)}) collective-permute-start(bf16[8,128,128]{2,1,0:T(8,128)(2,1)S(1)} %pad_maximum_fusion), channel_id=1, source_target_pairs={{0,64},{32,96},{64,0},{96,32},{128,192},{160,224},{192,128},{224,1... | collective-permute-start | bytes 786440 | tf_op jit(solution)/shard_map/ppermute | solution.py:43
  185.4 11.9 %collective-permute-start.11 = (bf16[16,128,128]{2,1,0:T(8,128)(2,1)S(1)}, bf16[16,128,128]{2,1,0:T(8,128)(2,1)S(1)}, u32[]{:S(2)}, u32[]{:S(2)}) collective-permute-start(bf16[16,128,128]{2,1,0:T(8,128)(2,1)S(1)} %get-tuple-element.13), channel_id=1, source_target_pairs={{0,32},{32,0},{64,96},{96,64},{128,160},{160,128},{192,224},{224,1... | collective-permute-start | bytes 1572872 | tf_op jit(solution)/shard_map/ppermute | solution.py:43
  217.9 9.2 %collective-permute-start.12 = (bf16[8,128,128]{2,1,0:T(8,128)(2,1)S(1)}, bf16[8,128,128]{2,1,0:T(8,128)(2,1)S(1)}, u32[]{:S(2)}, u32[]{:S(2)}) collective-permute-start(bf16[8,128,128]{2,1,0:T(8,128)(2,1)S(1)} %all_to_all.26.refs_4_), channel_id=1, source_target_pairs={{0,512},{32,544},{64,576},{96,608},{128,640},{160,672},{192,704},{... | collective-permute-start | bytes 786440 | tf_op jit(solution)/shard_map/ppermute | solution.py:48
  219.9 12.9 %collective-permute-start.14 = (bf16[8,128,128]{2,1,0:T(8,128)(2,1)S(1)}, bf16[8,128,128]{2,1,0:T(8,128)(2,1)S(1)}, u32[]{:S(2)}, u32[]{:S(2)}) collective-permute-start(bf16[8,128,128]{2,1,0:T(8,128)(2,1)S(1)} %all_to_all.26.refs_4_), channel_id=1, source_target_pairs={{0,32},{32,0},{64,96},{96,64},{128,160},{160,128},{192,224},{224,1... | collective-permute-start | bytes 786440 | tf_op jit(solution)/shard_map/ppermute | solution.py:48
  227.2 10.2 %collective-permute-start.13 = (bf16[8,128,128]{2,1,0:T(8,128)(2,1)S(1)}, bf16[8,128,128]{2,1,0:T(8,128)(2,1)S(1)}, u32[]{:S(2)}, u32[]{:S(2)}) collective-permute-start(bf16[8,128,128]{2,1,0:T(8,128)(2,1)S(1)} %collective-permute-done.12.refs_4_), channel_id=1, source_target_pairs={{0,32},{32,0},{64,96},{96,64},{128,160},{160,128},{192,224},{224,1... | collective-permute-start | bytes 786440 | tf_op jit(solution)/shard_map/ppermute | solution.py:48

commit v6 on v5

--- a/solution.py
+++ b/solution.py
@@ -15,7 +15,7 @@
 
 Z_GROUPS = [[grid_index(y, z, c) for z in range(Z)] for y in range(Y) for c in range(CORE)]
 YC_GROUPS = [[grid_index(y, z, c) for y in range(Y) for c in range(CORE)] for z in range(Z)]
-GRID_BITS = (16, 8, 4, 2, 1)
+GRID_BITS, NEAR_Z = (16, 8, 4, 2, 1), (4, 2, 6)
 X_BITS, X_FAR, Y_HI = (0, 1, 2, 3), (0, 4), (0, 8, 16, 24)
 
 
@@ -52,6 +52,12 @@
     near = jnp.stack([block, *(swap(block, "band", y) for y in Y_HI[1:])])
     half = jnp.concatenate([near, swap(near, "band", X_FAR[1])])
     return [half, *(swap(half, "band", x) for x in X_BITS[1:])]
+
+
+def gather_product(block):
+    quarter = gather_doubling(block, "grid", GRID_BITS[:2])
+    half = jnp.concatenate([quarter, *(swap(quarter, "grid", z) for z in NEAR_Z)])
+    return jnp.concatenate([half, swap(half, "grid", GRID_BITS[4])])
 
 
 def doubled_place(k, bits):
@@ -198,7 +204,7 @@
     blocks = jnp.asarray(blocks, jnp.int32) ^ lax.axis_index("band")
     sampled = place(gathered, take(placing.reshape(band_count, own), blocks).reshape(point_count))
     product = multiply(metric_parts, sampled)
-    products = gather_doubling(product, "grid", GRID_BITS).reshape(point_count, -1)
+    products = gather_product(product).reshape(point_count, -1)
     density = jnp.sum(partial_rows.astype(jnp.float32), axis=0) * (1.0 / NB)
     squared = (density * density).astype(jnp.bfloat16)
     squared = exchange_band(spread(squared, band_count))
@@ -229,6 +235,4 @@
 
 def solution(mesh):
     placed = (P("grid", "band"), P(), P("grid", None), P("grid", "band"))
-    return jax.shard_map(
-        shards, mesh=mesh, in_specs=placed, out_specs=P("grid", "band"), check_vma=False
-    )
+    return jax.shard_map(shards, mesh=mesh, in_specs=placed, out_specs=P("grid", "band"), check_vma=False)

time: 241 us -> 239 us (level)
  the two profiles are of different devices: /device:TPU:13 before, /device:TPU:1 now
where the time goes in v6:
time: 239 us; the launch traced here: 235 us
  starting transfers between devices  80.1 us (34%)
  waiting for transfers between devices  71.4 us (30%)
  blocking collectives  42.8 us (18%)
  Pallas kernels  20.8 us (9%)
  other arithmetic  12.9 us (5%)
  local copies, waits for them, and re-layouts  5.08 us (2%)
    ppermute x14, waiting for transfers between devices, swap(): lax.ppermute(x, axis, [(i, i ^ bit) for i in range(lax.axis_size(axis))])  54.3 us
    ppermute x14, starting transfers between devices, swap(): lax.ppermute(x, axis, [(i, i ^ bit) for i in range(lax.axis_size(axis))])  53.6 us
    all_to_all x2, blocking collectives, gather_z(): lax.all_to_all(spread(x, Z), 'grid', 0, 0, axis_index_groups=Z_GROUPS, ti...  42.8 us
    all_to_all x2, starting transfers between devices, exchange_band(): return lax.all_to_all(blocks, 'band', 0, 0, tiled=True)  16.6 us
    pallas_call x2, Pallas kernels, place(): pl.pallas_call(place_kernel, out_shape=jax.ShapeDtypeStruct(rows.shape, r...  10.7 us
    pallas_call x4, Pallas kernels, apply(): pl.pallas_call(apply_kernel, out_shape=jax.ShapeDtypeStruct((rows, column...  9.71 us
    ppermute x2, waiting for transfers between devices, gather_doubling(): lax.ppermute(x, axis, [(j, j ^ bit) for j in range(count)])  9.54 us
    all_to_all x1, waiting for transfers between devices, gather_yc(): lax.all_to_all(spread(along_z, Y * CORE), 'grid', 0, 0, axis_index_groups...  7.54 us
  transfers between devices with their start and end apart: 19, of which 10 were waited for; matrix products, arithmetic and copies ran while one was open for 4% of the time, Pallas kernels for 8%

profile of v6, /device:TPU:1, one launch (start us, length us, event | category | flops | bytes accessed | tf_op | source)
XLA Modules:
  0.0 235.4 jit_solution(3303822448476394223)
XLA Ops:
  0.0 0.7 broadcast_xor_fusion
  0.7 5.9 %sort.30 = (s32[4096]{0:T(1024)S(1)}, s32[4096]{0:T(1024)S(1)}) sort(s32[4096]{0:T(1024)} %param.6, s32[4096]{0:T(1024)S(1)} %iota.5), dimensions={0}, to_apply=%region_0.0 | sort | flops 49152 | bytes 65536 | tf_op jit(solution)/shard_map/sort | solution.py:189
  6.7 0.7 gather_fusion
  7.4 27.5 %all_to_all.25 = bf16[8,128,128]{2,1,0:T(8,128)(2,1)S(1)} all-to-all(bf16[8,128,128]{2,1,0:T(8,128)(2,1)S(1)} %broadcast_in_dim.43), channel_id=1, replica_groups={{0,64,128,192,256,320,384,448},{32,96,160,224,288,352,416,480},{512,576..., dimensions={0} | all-to-all | bytes 524288 | tf_op jit(solution)/shard_map/all_to_all | solution.py:27
  35.0 1.2 broadcast_in_dim.44
  36.2 5.8 %all-to-all-start.1 = ((bf16[4,8,128,128]{3,2,1,0:T(8,128)(2,1)}), bf16[4,8,128,128]{3,2,1,0:T(8,128)(2,1)S(1)}, u32[]{:S(2)}, u32[]{:S(2)}) async-start(bf16[4,8,128,128]{3,2,1,0:T(8,128)(2,1)} %broadcast_in_dim.44), calls=%async_computation.1 | async-start | bytes 2097152 | tf_op jit(solution)/shard_map/all_to_all | solution.py:31
  42.0 5.8 %sort.31 = (s32[4096]{0:T(1024)}, s32[4096]{0:T(1024)S(1)}) sort(s32[4096]{0:T(1024)S(1)} %get-tuple-element.9, s32[4096]{0:T(1024)S(1)} %iota.6), dimensions={0}, to_apply=%region_1.2 | sort | flops 49152 | bytes 65536 | tf_op jit(solution)/shard_map/sort | solution.py:195
  47.9 7.5 %all-to-all-done.1 = bf16[4,8,128,128]{3,2,1,0:T(8,128)(2,1)S(1)} async-done(((bf16[4,8,128,128]{3,2,1,0:T(8,128)(2,1)}), bf16[4,8,128,128]{3,2,1,0:T(8,128)(2,1)S(1)}, u32[]{:S(2)}, u32[]{:S(2)}) %all-to-all-start.1) | async-done | bytes 1048608 | tf_op jit(solution)/shard_map/all_to_all | solution.py:31
  55.5 0.7 gather_fusion.1
  56.2 1.4 convolution_convert_fusion
  57.6 12.6 %all-to-all-start.2 = ((bf16[32,128,128]{2,1,0:T(8,128)(2,1)}), bf16[32,128,128]{2,1,0:T(8,128)(2,1)S(1)}, u32[]{:S(2)}, u32[]{:S(2)}) async-start(bf16[32,128,128]{2,1,0:T(8,128)(2,1)} %bitcast.2), calls=%async_computation.2 | async-start | bytes 2097152 | tf_op jit(solution)/shard_map/all_to_all | solution.py:36
  70.2 4.0 %collective-permute-start = (bf16[128,128]{1,0:T(8,128)(2,1)S(1)}, bf16[128,128]{1,0:T(8,128)(2,1)S(1)}, u32[]{:S(2)}, u32[]{:S(2)}) collective-permute-start(bf16[128,128]{1,0:T(8,128)(2,1)S(1)} %get-tuple-element.12), channel_id=1, source_target_pairs={{0,8},{1,9},{2,10},{3,11},{4,12},{5,13},{6,14},{7,15},{8,0},{9,1},... | collective-permute-start | bytes 98312 | tf_op jit(solution)/shard_map/ppermute | solution.py:48
  74.3 5.2 %collective-permute-start.1 = (bf16[128,128]{1,0:T(8,128)(2,1)S(1)}, bf16[128,128]{1,0:T(8,128)(2,1)S(1)}, u32[]{:S(2)}, u32[]{:S(2)}) collective-permute-start(bf16[128,128]{1,0:T(8,128)(2,1)S(1)} %get-tuple-element.12), channel_id=1, source_target_pairs={{0,16},{1,17},{2,18},{3,19},{4,20},{5,21},{6,22},{7,23},{8,24},{9,... | collective-permute-start | bytes 98312 | tf_op jit(solution)/shard_map/ppermute | solution.py:48
  79.5 2.1 collective-permute-start.2
  81.6 19.2 %collective-permute-done.1 = bf16[128,128]{1,0:T(8,128)(2,1)S(1)} collective-permute-done((bf16[128,128]{1,0:T(8,128)(2,1)S(1)}, bf16[128,128]{1,0:T(8,128)(2,1)S(1)}, u32[]{:S(2)}, u32[]{:S(2)}) %collective-permute-start.1) | collective-permute-done | bytes 32800 | tf_op jit(solution)/shard_map/ppermute | solution.py:48
  100.8 1.3 collective-permute-done.2
  102.2 6.3 %collective-permute-start.3 = (bf16[4,128,128]{2,1,0:T(8,128)(2,1)S(1)}, bf16[4,128,128]{2,1,0:T(8,128)(2,1)S(1)}, u32[]{:S(2)}, u32[]{:S(2)}) collective-permute-start(bf16[4,128,128]{2,1,0:T(8,128)(2,1)S(1)} %pad_maximum_fusion), channel_id=1, source_target_pairs={{0,4},{1,5},{2,6},{3,7},{4,0},{5,1},{6,2},{7,3},{8,12},{9,13},{10,... | collective-permute-start | bytes 393224 | tf_op jit(solution)/shard_map/ppermute | solution.py:48
  108.9 1.2 broadcast_in_dim.46
  110.1 4.0 %all-to-all-start.3 = ((bf16[32,128,128]{1,2,0:T(8,128)(2,1)}), bf16[32,128,128]{1,2,0:T(8,128)(2,1)S(1)}, u32[]{:S(2)}, u32[]{:S(2)}) async-start(bf16[32,128,128]{1,2,0:T(8,128)(2,1)} %broadcast_in_dim.46), calls=%async_computation.3 | async-start | bytes 2097152 | tf_op jit(solution)/shard_map/all_to_all | solution.py:36
  114.2 3.1 %collective-permute-start.4 = (bf16[8,128,128]{2,1,0:T(8,128)(2,1)S(1)}, bf16[8,128,128]{2,1,0:T(8,128)(2,1)S(1)}, u32[]{:S(2)}, u32[]{:S(2)}) collective-permute-start(bf16[8,128,128]{2,1,0:T(8,128)(2,1)S(1)} %constant_dynamic-update-slice_fusion.refs_0_), channel_id=1, source_target_pairs={{0,1},{1,0},{2,3},{3,2},{4,5},{5,4},{6,7},{7,6},{8,9},{9,8},{10,11... | collective-permute-start | bytes 786440 | tf_op jit(solution)/shard_map/ppermute | solution.py:48
  117.3 4.0 %collective-permute-start.5 = (bf16[8,128,128]{2,1,0:T(8,128)(2,1)S(1)}, bf16[8,128,128]{2,1,0:T(8,128)(2,1)S(1)}, u32[]{:S(2)}, u32[]{:S(2)}) collective-permute-start(bf16[8,128,128]{2,1,0:T(8,128)(2,1)S(1)} %constant_dynamic-update-slice_fusion.refs_0_), channel_id=1, source_target_pairs={{0,2},{1,3},{2,0},{3,1},{4,6},{5,7},{6,4},{7,5},{8,10},{9,11},{10,... | collective-permute-start | bytes 786440 | tf_op jit(solution)/shard_map/ppermute | solution.py:48
  121.3 2.8 %collective-permute-start.6 = (bf16[8,128,128]{2,1,0:T(8,128)(2,1)S(1)}, bf16[8,128,128]{2,1,0:T(8,128)(2,1)S(1)}, u32[]{:S(2)}, u32[]{:S(2)}) collective-permute-start(bf16[8,128,128]{2,1,0:T(8,128)(2,1)S(1)} %constant_dynamic-update-slice_fusion.refs_0_), channel_id=1, source_target_pairs={{0,3},{1,2},{2,1},{3,0},{4,7},{5,6},{6,5},{7,4},{8,11},{9,10},{10,... | collective-permute-start | bytes 786440 | tf_op jit(solution)/shard_map/ppermute | solution.py:48
  124.1 0.6 gather_fusion.2
  124.7 5.4 %place_rows.2.refs_4_ = bf16[4096,128]{1,0:T(8,128)(2,1)S(1)} custom-call(s32[4096]{0:T(1024)S(1)} %bitcast.42, bf16[4096,128]{1,0:T(8,128)(2,1)S(1)} %bitcast.36), custom_call_target="tpu_custom_call" | custom-call | bytes 6291456 | tf_op jit(solution)/shard_map/place_rows/pallas_call | solution.py:89
  130.1 19.4 %collective-permute-done.4.refs_1_ = bf16[8,128,128]{2,1,0:T(8,128)(2,1)S(1)} collective-permute-done((bf16[8,128,128]{2,1,0:T(8,128)(2,1)S(1)}, bf16[8,128,128]{2,1,0:T(8,128)(2,1)S(1)}, u32[]{:S(2)}, u32[]{:S(2)}) %collective-permute-start.4) | collective-permute-done | bytes 262176 | tf_op jit(solution)/shard_map/ppermute | solution.py:48
  149.4 7.2 %collective-permute-done.6.refs_3_ = bf16[8,128,128]{2,1,0:T(8,128)(2,1)S(1)} collective-permute-done((bf16[8,128,128]{2,1,0:T(8,128)(2,1)S(1)}, bf16[8,128,128]{2,1,0:T(8,128)(2,1)S(1)}, u32[]{:S(2)}, u32[]{:S(2)}) %collective-permute-start.6) | collective-permute-done | bytes 262176 | tf_op jit(solution)/shard_map/ppermute | solution.py:48
  156.6 0.4 multiply_metric.1
  157.0 1.9 collective-permute-start.7
  159.0 2.7 %collective-permute-done.7 = bf16[1,128,128]{2,1,0:T(8,128)(2,1)S(1)} collective-permute-done((bf16[1,128,128]{2,1,0:T(8,128)(2,1)S(1)}, bf16[1,128,128]{2,1,0:T(8,128)(2,1)S(1)}, u32[]{:S(2)}, u32[]{:S(2)}) %collective-permute-start.7) | collective-permute-done | bytes 32800 | tf_op jit(solution)/shard_map/ppermute | solution.py:43
  161.7 2.2 collective-permute-start.8
  163.9 6.8 %collective-permute-done.8 = bf16[2,128,128]{2,1,0:T(8,128)(2,1)S(1)} collective-permute-done((bf16[2,128,128]{2,1,0:T(8,128)(2,1)S(1)}, bf16[2,128,128]{2,1,0:T(8,128)(2,1)S(1)}, u32[]{:S(2)}, u32[]{:S(2)}) %collective-permute-start.8) | collective-permute-done | bytes 65568 | tf_op jit(solution)/shard_map/ppermute | solution.py:43
  170.8 1.9 collective-permute-start.9
  172.7 2.5 %collective-permute-start.10 = (bf16[4,128,128]{2,1,0:T(8,128)(2,1)S(1)}, bf16[4,128,128]{2,1,0:T(8,128)(2,1)S(1)}, u32[]{:S(2)}, u32[]{:S(2)}) collective-permute-start(bf16[4,128,128]{2,1,0:T(8,128)(2,1)S(1)} %pad_maximum_fusion.1), channel_id=1, source_target_pairs={{0,64},{32,96},{64,0},{96,32},{128,192},{160,224},{192,128},{224,1... | collective-permute-start | bytes 393224 | tf_op jit(solution)/shard_map/ppermute | solution.py:48
  175.2 4.8 %collective-permute-start.11 = (bf16[4,128,128]{2,1,0:T(8,128)(2,1)S(1)}, bf16[4,128,128]{2,1,0:T(8,128)(2,1)S(1)}, u32[]{:S(2)}, u32[]{:S(2)}) collective-permute-start(bf16[4,128,128]{2,1,0:T(8,128)(2,1)S(1)} %pad_maximum_fusion.1), channel_id=1, source_target_pairs={{0,192},{32,224},{64,128},{96,160},{128,64},{160,96},{192,0},{224,... | collective-permute-start | bytes 393224 | tf_op jit(solution)/shard_map/ppermute | solution.py:48
  180.3 3.6 %collective-permute-done.11 = bf16[4,128,128]{2,1,0:T(8,128)(2,1)S(1)} collective-permute-done((bf16[4,128,128]{2,1,0:T(8,128)(2,1)S(1)}, bf16[4,128,128]{2,1,0:T(8,128)(2,1)S(1)}, u32[]{:S(2)}, u32[]{:S(2)}) %collective-permute-start.11) | collective-permute-done | bytes 131104 | tf_op jit(solution)/shard_map/ppermute | solution.py:48
  183.9 6.4 %collective-permute-start.12 = (bf16[16,128,128]{2,1,0:T(8,128)(2,1)S(1)}, bf16[16,128,128]{2,1,0:T(8,128)(2,1)S(1)}, u32[]{:S(2)}, u32[]{:S(2)}) collective-permute-start(bf16[16,128,128]{2,1,0:T(8,128)(2,1)S(1)} %get-tuple-element.13), channel_id=1, source_target_pairs={{0,32},{32,0},{64,96},{96,64},{128,160},{160,128},{192,224},{224,1... | collective-permute-start | bytes 1572872 | tf_op jit(solution)/shard_map/ppermute | solution.py:48
  190.5 1.4 collective-permute-done.12
  191.9 5.4 %place_rows.3 = bf16[4096,128]{1,0:T(8,128)(2,1)S(1)} custom-call(s32[4096]{0:T(1024)S(1)} %fusion.18.index_ref, bf16[4096,128]{1,0:T(8,128)(2,1)S(1)} %bitcast.38), custom_call_target="tpu_custom_call" | custom-call | bytes 6291456 | tf_op jit(solution)/shard_map/place_rows/pallas_call | solution.py:89
  197.3 0.4 fusion
  197.8 15.3 %all_to_all.26.refs_4_ = bf16[8,128,128]{2,1,0:T(8,128)(2,1)S(1)} all-to-all(bf16[8,128,128]{2,1,0:T(8,128)(2,1)S(1)} %broadcast_in_dim.49), channel_id=1, replica_groups={{0,64,128,192,256,320,384,448},{32,96,160,224,288,352,416,480},{512,576..., dimensions={0} | all-to-all | bytes 524288 | tf_op jit(solution)/shard_map/all_to_all | solution.py:27
  213.1 1.9 collective-permute-start.13
  215.0 3.9 %collective-permute-start.15 = (bf16[8,128,128]{2,1,0:T(8,128)(2,1)S(1)}, bf16[8,128,128]{2,1,0:T(8,128)(2,1)S(1)}, u32[]{:S(2)}, u32[]{:S(2)}) collective-permute-start(bf16[8,128,128]{2,1,0:T(8,128)(2,1)S(1)} %all_to_all.26.refs_4_), channel_id=1, source_target_pairs={{0,32},{32,0},{64,96},{96,64},{128,160},{160,128},{192,224},{224,1... | collective-permute-start | bytes 786440 | tf_op jit(solution)/shard_map/ppermute | solution.py:48
  218.9 2.2 collective-permute-done.13.refs_4_
  221.1 4.5 %collective-permute-start.14 = (bf16[8,128,128]{2,1,0:T(8,128)(2,1)S(1)}, bf16[8,128,128]{2,1,0:T(8,128)(2,1)S(1)}, u32[]{:S(2)}, u32[]{:S(2)}) collective-permute-start(bf16[8,128,128]{2,1,0:T(8,128)(2,1)S(1)} %collective-permute-done.13.refs_4_), channel_id=1, source_target_pairs={{0,32},{32,0},{64,96},{96,64},{128,160},{160,128},{192,224},{224,1... | collective-permute-start | bytes 786440 | tf_op jit(solution)/shard_map/ppermute | solution.py:48
  225.7 2.3 apply_theta.4.refs_5_
  227.9 2.3 apply_theta.5.refs_5_
  230.2 2.3 apply_theta.6.refs_5_
  232.5 2.9 %apply_theta.7 = bf16[1024,128]{1,0:T(8,128)(2,1)} custom-call(s32[1]{0:T(128)} %bitcast._, bf16[1024,4096]{1,0:T(8,128)(2,1)} %refs_3_.7, bf16[1024,4096]{1,0:T(8,128)(2,1)} %refs_3_.7, bf16[1024,4096]{1,0:T(8,128)(2,1)} %refs_3_.7, bf16[1024,4096]{1,0:T(8,128)(2,1)} %refs_3_.7, bf16[8,128,128]{2,1,0:T(8,128)(2,1)S(1)} %collective-permute-done.14.refs_4_, ...), custom_call_target="tpu_custom_call" | custom-call | flops 268435456 | bytes 2097152 | tf_op jit(solution)/shard_map/apply_theta/pallas_call | solution.py:156
  (44 shorter events, 1.2 us)
Async XLA Ops:
  0.0 6.7 %copy-start = (bf16[1024,128]{1,0:T(8,128)(2,1)S(1)}, bf16[1024,128]{1,0:T(8,128)(2,1)}, u32[]{:S(2)}) copy-start(bf16[1024,128]{1,0:T(8,128)(2,1)} %param.5) | copy-start | bytes 786436
  36.2 19.3 %all-to-all-start.1 = ((bf16[4,8,128,128]{3,2,1,0:T(8,128)(2,1)}), bf16[4,8,128,128]{3,2,1,0:T(8,128)(2,1)S(1)}, u32[]{:S(2)}, u32[]{:S(2)}) async-start(bf16[4,8,128,128]{3,2,1,0:T(8,128)(2,1)} %broadcast_in_dim.44), calls=%async_computation.1 | async-start | bytes 2097152 | tf_op jit(solution)/shard_map/all_to_all | solution.py:31
  56.2 14.0 %copy-start.1 = (f32[128,128]{1,0:T(8,128)S(1)}, f32[128,128]{1,0:T(8,128)}, u32[]{:S(2)}) copy-start(f32[128,128]{1,0:T(8,128)} %param.8) | copy-start | bytes 196612
  57.6 51.0 %all-to-all-start.2 = ((bf16[32,128,128]{2,1,0:T(8,128)(2,1)}), bf16[32,128,128]{2,1,0:T(8,128)(2,1)S(1)}, u32[]{:S(2)}, u32[]{:S(2)}) async-start(bf16[32,128,128]{2,1,0:T(8,128)(2,1)} %bitcast.2), calls=%async_computation.2 | async-start | bytes 2097152 | tf_op jit(solution)/shard_map/all_to_all | solution.py:36
  70.2 11.4 %collective-permute-start = (bf16[128,128]{1,0:T(8,128)(2,1)S(1)}, bf16[128,128]{1,0:T(8,128)(2,1)S(1)}, u32[]{:S(2)}, u32[]{:S(2)}) collective-permute-start(bf16[128,128]{1,0:T(8,128)(2,1)S(1)} %get-tuple-element.12), channel_id=1, source_target_pairs={{0,8},{1,9},{2,10},{3,11},{4,12},{5,13},{6,14},{7,15},{8,0},{9,1},... | collective-permute-start | bytes 98312 | tf_op jit(solution)/shard_map/ppermute | solution.py:48
  74.3 26.6 %collective-permute-start.1 = (bf16[128,128]{1,0:T(8,128)(2,1)S(1)}, bf16[128,128]{1,0:T(8,128)(2,1)S(1)}, u32[]{:S(2)}, u32[]{:S(2)}) collective-permute-start(bf16[128,128]{1,0:T(8,128)(2,1)S(1)} %get-tuple-element.12), channel_id=1, source_target_pairs={{0,16},{1,17},{2,18},{3,19},{4,20},{5,21},{6,22},{7,23},{8,24},{9,... | collective-permute-start | bytes 98312 | tf_op jit(solution)/shard_map/ppermute | solution.py:48
  79.5 22.7 %collective-permute-start.2 = (bf16[128,128]{1,0:T(8,128)(2,1)S(1)}, bf16[128,128]{1,0:T(8,128)(2,1)S(1)}, u32[]{:S(2)}, u32[]{:S(2)}) collective-permute-start(bf16[128,128]{1,0:T(8,128)(2,1)S(1)} %get-tuple-element.12), channel_id=1, source_target_pairs={{0,24},{1,25},{2,26},{3,27},{4,28},{5,29},{6,30},{7,31},{8,16},{9,... | collective-permute-start | bytes 98312 | tf_op jit(solution)/shard_map/ppermute | solution.py:48
  102.2 11.9 %collective-permute-start.3 = (bf16[4,128,128]{2,1,0:T(8,128)(2,1)S(1)}, bf16[4,128,128]{2,1,0:T(8,128)(2,1)S(1)}, u32[]{:S(2)}, u32[]{:S(2)}) collective-permute-start(bf16[4,128,128]{2,1,0:T(8,128)(2,1)S(1)} %pad_maximum_fusion), channel_id=1, source_target_pairs={{0,4},{1,5},{2,6},{3,7},{4,0},{5,1},{6,2},{7,3},{8,12},{9,13},{10,... | collective-permute-start | bytes 393224 | tf_op jit(solution)/shard_map/ppermute | solution.py:48
  110.1 87.2 %all-to-all-start.3 = ((bf16[32,128,128]{1,2,0:T(8,128)(2,1)}), bf16[32,128,128]{1,2,0:T(8,128)(2,1)S(1)}, u32[]{:S(2)}, u32[]{:S(2)}) async-start(bf16[32,128,128]{1,2,0:T(8,128)(2,1)} %broadcast_in_dim.46), calls=%async_computation.3 | async-start | bytes 2097152 | tf_op jit(solution)/shard_map/all_to_all | solution.py:36
  114.2 35.3 %collective-permute-start.4 = (bf16[8,128,128]{2,1,0:T(8,128)(2,1)S(1)}, bf16[8,128,128]{2,1,0:T(8,128)(2,1)S(1)}, u32[]{:S(2)}, u32[]{:S(2)}) collective-permute-start(bf16[8,128,128]{2,1,0:T(8,128)(2,1)S(1)} %constant_dynamic-update-slice_fusion.refs_0_), channel_id=1, source_target_pairs={{0,1},{1,0},{2,3},{3,2},{4,5},{5,4},{6,7},{7,6},{8,9},{9,8},{10,11... | collective-permute-start | bytes 786440 | tf_op jit(solution)/shard_map/ppermute | solution.py:48
  117.3 32.1 %collective-permute-start.5 = (bf16[8,128,128]{2,1,0:T(8,128)(2,1)S(1)}, bf16[8,128,128]{2,1,0:T(8,128)(2,1)S(1)}, u32[]{:S(2)}, u32[]{:S(2)}) collective-permute-start(bf16[8,128,128]{2,1,0:T(8,128)(2,1)S(1)} %constant_dynamic-update-slice_fusion.refs_0_), channel_id=1, source_target_pairs={{0,2},{1,3},{2,0},{3,1},{4,6},{5,7},{6,4},{7,5},{8,10},{9,11},{10,... | collective-permute-start | bytes 786440 | tf_op jit(solution)/shard_map/ppermute | solution.py:48
  121.3 35.3 %collective-permute-start.6 = (bf16[8,128,128]{2,1,0:T(8,128)(2,1)S(1)}, bf16[8,128,128]{2,1,0:T(8,128)(2,1)S(1)}, u32[]{:S(2)}, u32[]{:S(2)}) collective-permute-start(bf16[8,128,128]{2,1,0:T(8,128)(2,1)S(1)} %constant_dynamic-update-slice_fusion.refs_0_), channel_id=1, source_target_pairs={{0,3},{1,2},{2,1},{3,0},{4,7},{5,6},{6,5},{7,4},{8,11},{9,10},{10,... | collective-permute-start | bytes 786440 | tf_op jit(solution)/shard_map/ppermute | solution.py:48
  157.0 4.7 %collective-permute-start.7 = (bf16[1,128,128]{2,1,0:T(8,128)(2,1)S(1)}, bf16[1,128,128]{2,1,0:T(8,128)(2,1)S(1)}, u32[]{:S(2)}, u32[]{:S(2)}) collective-permute-start(bf16[1,128,128]{2,1,0:T(8,128)(2,1)S(1)} %bitcast.39), channel_id=1, source_target_pairs={{0,512},{32,544},{64,576},{96,608},{128,640},{160,672},{192,704},{... | collective-permute-start | bytes 98312 | tf_op jit(solution)/shard_map/ppermute | solution.py:43
  161.7 9.0 %collective-permute-start.8 = (bf16[2,128,128]{2,1,0:T(8,128)(2,1)S(1)}, bf16[2,128,128]{2,1,0:T(8,128)(2,1)S(1)}, u32[]{:S(2)}, u32[]{:S(2)}) collective-permute-start(bf16[2,128,128]{2,1,0:T(8,128)(2,1)S(1)} %pad_maximum_fusion.2), channel_id=1, source_target_pairs={{0,256},{32,288},{64,320},{96,352},{128,384},{160,416},{192,448},{... | collective-permute-start | bytes 196616 | tf_op jit(solution)/shard_map/ppermute | solution.py:43
  170.8 9.4 %collective-permute-start.9 = (bf16[4,128,128]{2,1,0:T(8,128)(2,1)S(1)}, bf16[4,128,128]{2,1,0:T(8,128)(2,1)S(1)}, u32[]{:S(2)}, u32[]{:S(2)}) collective-permute-start(bf16[4,128,128]{2,1,0:T(8,128)(2,1)S(1)} %pad_maximum_fusion.1), channel_id=1, source_target_pairs={{0,128},{32,160},{64,192},{96,224},{128,0},{160,32},{192,64},{224,... | collective-permute-start | bytes 393224 | tf_op jit(solution)/shard_map/ppermute | solution.py:48
  172.7 7.5 %collective-permute-start.10 = (bf16[4,128,128]{2,1,0:T(8,128)(2,1)S(1)}, bf16[4,128,128]{2,1,0:T(8,128)(2,1)S(1)}, u32[]{:S(2)}, u32[]{:S(2)}) collective-permute-start(bf16[4,128,128]{2,1,0:T(8,128)(2,1)S(1)} %pad_maximum_fusion.1), channel_id=1, source_target_pairs={{0,64},{32,96},{64,0},{96,32},{128,192},{160,224},{192,128},{224,1... | collective-permute-start | bytes 393224 | tf_op jit(solution)/shard_map/ppermute | solution.py:48
  175.2 8.6 %collective-permute-start.11 = (bf16[4,128,128]{2,1,0:T(8,128)(2,1)S(1)}, bf16[4,128,128]{2,1,0:T(8,128)(2,1)S(1)}, u32[]{:S(2)}, u32[]{:S(2)}) collective-permute-start(bf16[4,128,128]{2,1,0:T(8,128)(2,1)S(1)} %pad_maximum_fusion.1), channel_id=1, source_target_pairs={{0,192},{32,224},{64,128},{96,160},{128,64},{160,96},{192,0},{224,... | collective-permute-start | bytes 393224 | tf_op jit(solution)/shard_map/ppermute | solution.py:48
  183.9 7.9 %collective-permute-start.12 = (bf16[16,128,128]{2,1,0:T(8,128)(2,1)S(1)}, bf16[16,128,128]{2,1,0:T(8,128)(2,1)S(1)}, u32[]{:S(2)}, u32[]{:S(2)}) collective-permute-start(bf16[16,128,128]{2,1,0:T(8,128)(2,1)S(1)} %get-tuple-element.13), channel_id=1, source_target_pairs={{0,32},{32,0},{64,96},{96,64},{128,160},{160,128},{192,224},{224,1... | collective-permute-start | bytes 1572872 | tf_op jit(solution)/shard_map/ppermute | solution.py:48
  213.1 8.0 %collective-permute-start.13 = (bf16[8,128,128]{2,1,0:T(8,128)(2,1)S(1)}, bf16[8,128,128]{2,1,0:T(8,128)(2,1)S(1)}, u32[]{:S(2)}, u32[]{:S(2)}) collective-permute-start(bf16[8,128,128]{2,1,0:T(8,128)(2,1)S(1)} %all_to_all.26.refs_4_), channel_id=1, source_target_pairs={{0,512},{32,544},{64,576},{96,608},{128,640},{160,672},{192,704},{... | collective-permute-start | bytes 786440 | tf_op jit(solution)/shard_map/ppermute | solution.py:48
  215.0 12.9 %collective-permute-start.15 = (bf16[8,128,128]{2,1,0:T(8,128)(2,1)S(1)}, bf16[8,128,128]{2,1,0:T(8,128)(2,1)S(1)}, u32[]{:S(2)}, u32[]{:S(2)}) collective-permute-start(bf16[8,128,128]{2,1,0:T(8,128)(2,1)S(1)} %all_to_all.26.refs_4_), channel_id=1, source_target_pairs={{0,32},{32,0},{64,96},{96,64},{128,160},{160,128},{192,224},{224,1... | collective-permute-start | bytes 786440 | tf_op jit(solution)/shard_map/ppermute | solution.py:48
  221.1 11.4 %collective-permute-start.14 = (bf16[8,128,128]{2,1,0:T(8,128)(2,1)S(1)}, bf16[8,128,128]{2,1,0:T(8,128)(2,1)S(1)}, u32[]{:S(2)}, u32[]{:S(2)}) collective-permute-start(bf16[8,128,128]{2,1,0:T(8,128)(2,1)S(1)} %collective-permute-done.13.refs_4_), channel_id=1, source_target_pairs={{0,32},{32,0},{64,96},{96,64},{128,160},{160,128},{192,224},{224,1... | collective-permute-start | bytes 786440 | tf_op jit(solution)/shard_map/ppermute | solution.py:48
